TPU v7x, 256 devices: a whole 4x4x8 slice. The times are simulated.
256 devices in a mesh: seq: 64 (over y, z_hi, x, core), dp: 4 (over z_lo).
Axes of the slice: x: 4, y: 4, z: 8 (z_hi: 2, z_lo: 4; z = z_hi * 4 + z_lo), core: 2. Of those that a mesh axis runs over, the one named last changes fastest.
Arguments:
- query: bfloat16 [4, 8192, 2048], P('dp', 'seq'), may hold values from -6 to 6
- keys: bfloat16 [4, 8192, 512], P('dp', 'seq'), may hold values from -6 to 6
- values: bfloat16 [4, 8192, 512], P('dp', 'seq'), may hold values from -6 to 6
- out_grad: bfloat16 [4, 8192, 2048], P('dp', 'seq'), may hold values from -16 to 16
- normed_input: bfloat16 [4, 8192, 4096], P('dp', 'seq'), may hold values from -16 to 16
- q_start: int32 [8], P('dp'), may hold values from 2048 to 3071, as said below
- q_len: int32 [8], P('dp'), may hold values from 1 to 512, as said below
Outputs:
- q_grad: bfloat16 [4, 8192, 2048], P('dp', 'seq')
- k_grad: bfloat16 [4, 8192, 512], P('dp', 'seq')
- v_grad: bfloat16 [4, 8192, 512], P('dp', 'seq')
- kv_weight_grad: float32 [4096, 1024], P(('seq', 'dp'))
Inputs may be any that keep to these rules, and one draw needn't show every extreme that they name: `q_start`: the visual part of each sequence ends here. `q_len`: tokens after the question are padding.
All inputs are finite; a program needn't handle non-finite values.
Results may differ from a plain program's by a relative error of at most 0.013.
Values may be sent and summed in bfloat16 or wider, within the bound.
A program may use at most 128 MiB of HBM per device.

v0:
```python
import math

import jax
import jax.numpy as jnp
from jax import lax
from jax.sharding import PartitionSpec as P

HEADS = 16
KV_HEADS = 4
HEAD_DIM = 128


def local(query, keys, values, out_grad, normed_input, q_start, q_len):
    seq_count = lax.axis_size("seq")
    tokens_dev = query.shape[1]
    repeat_by = HEADS // KV_HEADS
    classes = max(1, seq_count // HEADS)
    heads_dev = HEADS * classes // seq_count
    head_groups = seq_count // classes
    class_tokens = tokens_dev // classes
    seq_len = tokens_dev * seq_count // 2
    group_tokens = tokens_dev * seq_count
    width_dev = heads_dev * HEAD_DIM
    my_class = lax.axis_index("seq") // head_groups
    score_scale = 1.0 / math.sqrt(HEAD_DIM)

    def to_units(array):
        return array.reshape(class_tokens, seq_count, width_dev)

    query_units = to_units(query[0])
    grad_units = to_units(out_grad[0])
    key_wide = jnp.repeat(
        keys[0].reshape(tokens_dev, KV_HEADS, HEAD_DIM), repeat_by, axis=1
    ).reshape(tokens_dev, HEADS * HEAD_DIM)
    value_wide = jnp.repeat(
        values[0].reshape(tokens_dev, KV_HEADS, HEAD_DIM), repeat_by, axis=1
    ).reshape(tokens_dev, HEADS * HEAD_DIM)
    wide_shape = (tokens_dev, classes, head_groups, width_dev)
    key_units = jnp.broadcast_to(
        key_wide.reshape(tokens_dev, 1, head_groups, width_dev), wide_shape
    ).reshape(tokens_dev, seq_count, width_dev)
    value_units = jnp.broadcast_to(
        value_wide.reshape(tokens_dev, 1, head_groups, width_dev), wide_shape
    ).reshape(tokens_dev, seq_count, width_dev)
    query_got, grad_got, key_got, value_got = (
        lax.all_to_all(query_units, "seq", split_axis=1, concat_axis=0, tiled=True),
        lax.all_to_all(grad_units, "seq", split_axis=1, concat_axis=0, tiled=True),
        lax.all_to_all(key_units, "seq", split_axis=1, concat_axis=0, tiled=True),
        lax.all_to_all(value_units, "seq", split_axis=1, concat_axis=0, tiled=True),
    )
    block_rows = min(512, seq_len // classes)
    blocks_seq = seq_len // classes // block_rows
    key_pos = jnp.arange(seq_len, dtype=jnp.int32)

    def one_block(block_idx, carry):
        query_acc, key_acc, value_acc = carry
        seq_idx = block_idx // blocks_seq
        first_row = block_idx * block_rows
        key_first = seq_idx * seq_len
        query_block = lax.dynamic_slice_in_dim(query_got, first_row, block_rows, 0)
        grad_block = lax.dynamic_slice_in_dim(grad_got, first_row, block_rows, 0)
        key_block = lax.dynamic_slice_in_dim(key_got, key_first, seq_len, 0)
        value_block = lax.dynamic_slice_in_dim(value_got, key_first, seq_len, 0)
        start_pos = lax.dynamic_index_in_dim(q_start, seq_idx, 0, keepdims=False)
        end_pos = start_pos + lax.dynamic_index_in_dim(q_len, seq_idx, 0, keepdims=False)
        query_pos = (
            (first_row + jnp.arange(block_rows, dtype=jnp.int32)) * classes + my_class - key_first
        )
        visible = (key_pos[None, :] < end_pos) & (
            (key_pos[None, :] <= query_pos[:, None]) | (key_pos[None, :] < start_pos)
        )
        scores = (
            jnp.einsum("qhd,khd->hqk", query_block, key_block, preferred_element_type=jnp.float32)
            * score_scale
        )
        scores = jnp.where(visible[None], scores, -jnp.inf)
        row_max = jnp.max(scores, axis=-1, keepdims=True)
        exponent = jnp.where(visible[None], jnp.exp(scores - row_max), 0.0)
        probability = exponent / jnp.sum(exponent, axis=-1, keepdims=True)
        prob_low = probability.astype(jnp.bfloat16)
        dprob = jnp.einsum(
            "qhd,khd->hqk", grad_block, value_block, preferred_element_type=jnp.float32
        )
        row_delta = jnp.sum(probability * dprob, axis=-1, keepdims=True)
        dscore = (probability * (dprob - row_delta) * score_scale).astype(jnp.bfloat16)
        query_grad = jnp.einsum(
            "hqk,khd->qhd", dscore, key_block, preferred_element_type=jnp.float32
        ).astype(jnp.bfloat16)
        query_acc = lax.dynamic_update_slice_in_dim(query_acc, query_grad, first_row, 0)
        key_part = lax.dynamic_slice_in_dim(key_acc, key_first, seq_len, 0) + jnp.einsum(
            "hqk,qhd->khd", dscore, query_block, preferred_element_type=jnp.float32
        )
        value_part = lax.dynamic_slice_in_dim(value_acc, key_first, seq_len, 0) + jnp.einsum(
            "hqk,qhd->khd", prob_low, grad_block, preferred_element_type=jnp.float32
        )
        key_acc = lax.dynamic_update_slice_in_dim(key_acc, key_part, key_first, 0)
        value_acc = lax.dynamic_update_slice_in_dim(value_acc, value_part, key_first, 0)
        return (query_acc, key_acc, value_acc)

    start_state = (
        jnp.zeros((seq_count * class_tokens, heads_dev, HEAD_DIM), jnp.bfloat16),
        jnp.zeros((group_tokens, heads_dev, HEAD_DIM), jnp.float32),
        jnp.zeros((group_tokens, heads_dev, HEAD_DIM), jnp.float32),
    )
    query_acc, key_acc, value_acc = lax.fori_loop(0, 2 * blocks_seq, one_block, start_state)
    query_back = lax.all_to_all(
        query_acc.reshape(seq_count, class_tokens, 1, width_dev),
        "seq",
        split_axis=0,
        concat_axis=2,
        tiled=True,
    )
    query_grad_out = query_back.reshape(tokens_dev, HEADS * HEAD_DIM)
    key_back, value_back = (
        lax.all_to_all(
            key_acc.reshape(seq_count, tokens_dev, 1, width_dev).astype(jnp.bfloat16),
            "seq",
            split_axis=0,
            concat_axis=2,
            tiled=True,
        ).astype(jnp.float32),
        lax.all_to_all(
            value_acc.reshape(seq_count, tokens_dev, 1, width_dev).astype(jnp.bfloat16),
            "seq",
            split_axis=0,
            concat_axis=2,
            tiled=True,
        ).astype(jnp.float32),
    )
    key_grad_out = (
        key_back.reshape(tokens_dev, classes, KV_HEADS, repeat_by, HEAD_DIM)
        .sum(axis=(1, 3))
        .astype(jnp.bfloat16)
        .reshape(tokens_dev, KV_HEADS * HEAD_DIM)
    )
    value_grad_out = (
        value_back.reshape(tokens_dev, classes, KV_HEADS, repeat_by, HEAD_DIM)
        .sum(axis=(1, 3))
        .astype(jnp.bfloat16)
        .reshape(tokens_dev, KV_HEADS * HEAD_DIM)
    )
    joined = jnp.concatenate([key_grad_out, value_grad_out], axis=1)
    hidden_rows = normed_input[0]
    weight_out = lax.psum_scatter(
        jnp.einsum("tr,tc->rc", hidden_rows, joined, preferred_element_type=jnp.float32),
        ("seq", "dp"),
        scatter_dimension=0,
        tiled=True,
    )
    return (query_grad_out[None], key_grad_out[None], value_grad_out[None], weight_out)


def solution(mesh):
    in_specs = (
        P("dp", "seq", None),
        P("dp", "seq", None),
        P("dp", "seq", None),
        P("dp", "seq", None),
        P("dp", "seq", None),
        P("dp"),
        P("dp"),
    )
    out_specs = (
        P("dp", "seq", None),
        P("dp", "seq", None),
        P("dp", "seq", None),
        P(("seq", "dp"), None),
    )
    return jax.shard_map(local, mesh=mesh, in_specs=in_specs, out_specs=out_specs, check_vma=False)
```

profile of v0, /device:TPU:1, one launch (start us, length us, event | category | flops | bytes accessed | tf_op | source)
XLA Modules:
  0.0 1874.6 jit_solution(11580417287337845989)
XLA Ops:
  9.7 15.6 all-to-all-start.2
  27.8 15.3 all-to-all-done.2
  47.7 17.2 all-to-all-done.1
  67.0 7.7 all-to-all-start.3
  74.8 50.9 %all-to-all-done.3 = bf16[128,64,128]{2,0,1:T(8,128)(2,1)} async-done(((bf16[128,64,128]{2,0,1:T(8,128)(2,1)}), bf16[128,64,128]{2,0,1:T(8,128)(2,1)}, u32[]{:S(2)}, u32[]{:S(2)}) %all-to-all-start.3) | async-done | bytes 2097184 | tf_op jit(solution)/shard_map/all_to_all | solution.py:49
  127.7 7.5 all-to-all-start
  135.2 51.0 %all-to-all-done = bf16[128,64,128]{2,0,1:T(8,128)(2,1)S(1)} async-done(((bf16[128,64,128]{2,0,1:T(8,128)(2,1)}), bf16[128,64,128]{2,0,1:T(8,128)(2,1)S(1)}, u32[]{:S(2)}, u32[]{:S(2)}) %all-to-all-start) | async-done | bytes 2097184 | tf_op jit(solution)/shard_map/all_to_all | solution.py:48
  191.6 244.7 %while.21 = (s32[]{:T(128)}, bf16[2048,1,128]{2,0,1:T(8,128)(2,1)}, f32[8192,1,128]{2,0,1:T(8,128)}, f32[8192,1,128]{2,0,1:T(8,128)}, bf16[8192,1,128]{2,0,1:T(8...) while((s32[]{:T(128)}, bf16[2048,1,128]{2,0,1:T(8,128)(2,1)}, ...), condition=%wide.region_4.5_spmd.clone.clone, body=%wide.region_0.4_spmd.clone.clone.sunk | while | flops 2746294784 | bytes 167959120 | solution.py:105
  202.8 9.4 multiply_reduce_fusion.2
  212.3 10.0 multiply_convert_fusion.2
  264.0 9.4 multiply_reduce_fusion.2
  273.4 10.0 multiply_convert_fusion.2
  297.5 5.5 fusion.60
  325.2 9.4 multiply_reduce_fusion.2
  334.6 10.0 multiply_convert_fusion.2
  386.3 9.4 multiply_reduce_fusion.2
  395.7 10.0 multiply_convert_fusion.2
  451.9 25.2 %all-to-all-done.5 = bf16[64,128,1,128]{1,3,2,0:T(8,128)(2,1)} async-done(((bf16[64,128,1,128]{1,3,2,0:T(8,128)(2,1)}), bf16[64,128,1,128]{1,3,2,0:T(8,128)(2,1)}, u32[]{:S(2)}, u32[]{:S(2)}) %all-to-all-start.5) | async-done | bytes 2097184 | tf_op jit(solution)/shard_map/all_to_all | solution.py:115
  477.1 25.4 %all-to-all-start.6 = ((bf16[64,128,1,128]{1,3,2,0:T(8,128)(2,1)}), bf16[64,128,1,128]{1,3,2,0:T(8,128)(2,1)S(1)}, u32[]{:S(2)}, u32[]{:S(2)}) async-start(bf16[64,128,1,128]{1,3,2,0:T(8,128)(2,1)} %copy.50), calls=%async_computation.6 | async-start | bytes 4194304 | tf_op jit(solution)/shard_map/all_to_all | solution.py:122
  504.5 49.1 %all-to-all-done.6 = bf16[64,128,1,128]{1,3,2,0:T(8,128)(2,1)S(1)} async-done(((bf16[64,128,1,128]{1,3,2,0:T(8,128)(2,1)}), bf16[64,128,1,128]{1,3,2,0:T(8,128)(2,1)S(1)}, u32[]{:S(2)}, u32[]{:S(2)}) %all-to-all-start.6) | async-done | bytes 2097184 | tf_op jit(solution)/shard_map/all_to_all | solution.py:122
  553.9 8.1 convolution_bitcast_fusion.2
  561.9 17.4 copy.58
  580.4 18.6 all_to_all.105
  601.8 1265.9 %reduce-scatter.4.cloned.1.call-done = f32[16,1024]{1,0:T(8,128)} async-done(((f32[4096,1024]{1,0:T(8,128)}), f32[16,1024]{1,0:T(8,128)}) %reduce-scatter.4.cloned.1.call-update) | async-done | bytes 65552
  (152 shorter events, 197.0 us)
Async XLA Ops:
  7.2 546.7 %copy-start = (bf16[1,128,4096]{2,1,0:T(8,128)(2,1)S(1)}, bf16[1,128,4096]{2,1,0:T(8,128)(2,1)}, u32[]{:S(2)}) copy-start(bf16[1,128,4096]{2,1,0:T(8,128)(2,1)} %param.13) | copy-start | bytes 3145732
  7.2 40.5 %copy-start.8 = (bf16[1,128,512]{2,1,0:T(8,128)(2,1)S(1)}, bf16[1,128,512]{2,1,0:T(8,128)(2,1)}, u32[]{:S(2)}) copy-start(bf16[1,128,512]{2,1,0:T(8,128)(2,1)} %param.11) | copy-start | bytes 393220
  9.7 33.3 %all-to-all-start.2 = ((bf16[32,64,128]{2,0,1:T(8,128)(2,1)}), bf16[32,64,128]{2,0,1:T(8,128)(2,1)S(1)}, u32[]{:S(2)}, u32[]{:S(2)}) async-start(bf16[32,64,128]{2,0,1:T(8,128)(2,1)} %copy.40), calls=%async_computation.2 | async-start | bytes 1048576 | tf_op jit(solution)/shard_map/all_to_all | solution.py:47
  43.0 24.0 %copy-start.5 = (bf16[32,64,128]{2,0,1:T(8,128)(2,1)}, bf16[32,64,128]{2,0,1:T(8,128)(2,1)S(1)}, u32[]{:S(2)}) copy-start(bf16[32,64,128]{2,0,1:T(8,128)(2,1)S(1)} %all-to-all-done.2) | copy-start | bytes 1572868
  43.0 22.0 %all-to-all-start.1 = ((bf16[32,64,128]{2,0,1:T(8,128)(2,1)}), bf16[32,64,128]{2,0,1:T(8,128)(2,1)S(1)}, u32[]{:S(2)}, u32[]{:S(2)}) async-start(bf16[32,64,128]{2,0,1:T(8,128)(2,1)} %copy.39), calls=%async_computation.1 | async-start | bytes 1048576 | tf_op jit(solution)/shard_map/all_to_all | solution.py:46
  47.6 27.0 %copy-start.9 = (bf16[1,128,512]{2,1,0:T(8,128)(2,1)S(1)}, bf16[1,128,512]{2,1,0:T(8,128)(2,1)}, u32[]{:S(2)}) copy-start(bf16[1,128,512]{2,1,0:T(8,128)(2,1)} %param.10) | copy-start | bytes 393220
  65.0 60.8 %copy-start.6 = (bf16[32,64,128]{2,0,1:T(8,128)(2,1)}, bf16[32,64,128]{2,0,1:T(8,128)(2,1)S(1)}, u32[]{:S(2)}) copy-start(bf16[32,64,128]{2,0,1:T(8,128)(2,1)S(1)} %all-to-all-done.1) | copy-start | bytes 1572868
  67.0 58.7 %all-to-all-start.3 = ((bf16[128,64,128]{2,0,1:T(8,128)(2,1)}), bf16[128,64,128]{2,0,1:T(8,128)(2,1)}, u32[]{:S(2)}, u32[]{:S(2)}) async-start(bf16[128,64,128]{2,0,1:T(8,128)(2,1)} %bitcast.12), calls=%async_computation.3 | async-start | bytes 4194304 | tf_op jit(solution)/shard_map/all_to_all | solution.py:49
  127.7 58.5 %all-to-all-start = ((bf16[128,64,128]{2,0,1:T(8,128)(2,1)}), bf16[128,64,128]{2,0,1:T(8,128)(2,1)S(1)}, u32[]{:S(2)}, u32[]{:S(2)}) async-start(bf16[128,64,128]{2,0,1:T(8,128)(2,1)} %bitcast.133), calls=%async_computation | async-start | bytes 4194304 | tf_op jit(solution)/shard_map/all_to_all | solution.py:48
  186.2 5.4 copy-start.10
  186.2 5.4 copy-start.11
  191.6 7.0 copy-start.3
  245.0 4.1 copy-start.1
  252.8 7.0 copy-start.3
  306.1 4.1 copy-start.1
  313.9 7.0 copy-start.3
  367.3 4.1 copy-start.1
  371.4 3.7 copy-start.4
  375.1 7.0 copy-start.3
  428.5 4.1 copy-start.1
  432.5 3.7 copy-start.4
  441.5 35.6 %all-to-all-start.5 = ((bf16[64,128,1,128]{1,3,2,0:T(8,128)(2,1)}), bf16[64,128,1,128]{1,3,2,0:T(8,128)(2,1)}, u32[]{:S(2)}, u32[]{:S(2)}) async-start(bf16[64,128,1,128]{1,3,2,0:T(8,128)(2,1)} %copy.46), calls=%async_computation.5 | async-start | bytes 4194304 | tf_op jit(solution)/shard_map/all_to_all | solution.py:115
  477.1 76.4 %all-to-all-start.6 = ((bf16[64,128,1,128]{1,3,2,0:T(8,128)(2,1)}), bf16[64,128,1,128]{1,3,2,0:T(8,128)(2,1)S(1)}, u32[]{:S(2)}, u32[]{:S(2)}) async-start(bf16[64,128,1,128]{1,3,2,0:T(8,128)(2,1)} %copy.50), calls=%async_computation.6 | async-start | bytes 4194304 | tf_op jit(solution)/shard_map/all_to_all | solution.py:122
  502.5 1365.3 %reduce-scatter.4.cloned.1.call-start = ((), (), s32[]{:S(2)}) async-start(), calls=%async_computation.8 | async-start | bytes 16842752
  (7 other events, 20.7 us)
Sparse Core Ops, SparseCore 0:
  579.5 1288.1 reduce-scatter.3
where the time goes:
time: 1880 us; the launch traced here: 1870 us
  waiting for transfers between devices  1470 us (78%)
  local copies, waits for them, and re-layouts  120 us (6%)
  matrix products  109 us (6%)
  other arithmetic  66.8 us (4%)
  starting transfers between devices  65.9 us (4%)
    unnamed x2, waiting for transfers between devices  1270 us
    all_to_all x1, waiting for transfers between devices, local(): lax.all_to_all(key_units, 'seq', split_axis=1, concat_axis=0, tiled=True)  51 us
    all_to_all x1, waiting for transfers between devices, local(): lax.all_to_all(value_units, 'seq', split_axis=1, concat_axis=0, tiled=True)  50.9 us
    all_to_all x1, waiting for transfers between devices, local(): lax.all_to_all(value_acc.reshape(seq_count, tokens_dev, 1, width_dev).ast...  49.1 us
    convert_element_type x4, other arithmetic, one_block(): (probability * (dprob - row_delta) * score_scale).astype(jnp.bfloat16)  40.1 us
    dot_general x4, matrix products, one_block(): jnp.einsum('qhd,khd->hqk', grad_block, value_block, preferred_element_typ...  37.7 us
  transfers between devices with their start and end apart: 7, of which 7 were waited for; matrix products, arithmetic and copies ran while one was open for 1% of the time, Pallas kernels for 0%

commit v1 on v0

v1 whole, which is shorter than its diff:
```python
import math
import functools
import jax
import jax.numpy as jnp
from jax import lax
from jax.experimental import pallas as pl
from jax.experimental.pallas import tpu as pltpu
from jax.sharding import PartitionSpec as P

HEAD_DIM = 128
SCALE = 1.0 / math.sqrt(HEAD_DIM)
EXPC = SCALE * math.log2(math.e)
NEG = -1e30
F32 = jnp.float32
BF16 = jnp.bfloat16
CK = 512


def dot_nt(a, b):
    return lax.dot_general(a, b, (((1,), (1,)), ((), ())), preferred_element_type=F32)


def dot_nn(a, b):
    return lax.dot_general(a, b, (((1,), (0,)), ((), ())), preferred_element_type=F32)


def dot_tn(a, b):
    return lax.dot_general(a, b, (((0,), (0,)), ((), ())), preferred_element_type=F32)


def att_body(q_ref, g_ref, kv_ref, lim_ref, dq_ref, kvg_ref, s_ref, d_ref, dk_ref, dv_ref, kt_ref, variant):
    dk_ref[...] = jnp.zeros_like(dk_ref)
    dv_ref[...] = jnp.zeros_like(dv_ref)
    if variant == "kt":
        for j in range(7):
            kt_ref[:, j * CK:(j + 1) * CK] = kv_ref[pl.ds(j * CK, CK), 0:128].T

    def unit(h, yl, nk):
        cols = pl.ds(pl.multiple_of(h * 128, 128), 128)
        q = q_ref[yl, :, cols]
        g = g_ref[yl, :, cols]
        lim = lim_ref[yl]
        m = jnp.full((1, 256), NEG, F32)
        for j in range(nk):
            rows = pl.ds(j * CK, CK)
            s = dot_nt(kv_ref[rows, 0:128], q)
            if j >= 4:
                kpos = lax.broadcasted_iota(jnp.int32, (CK, 256), 0) + j * CK
                s = jnp.where(kpos < lim, s, NEG)
            s_ref[rows, :] = s
            m = jnp.maximum(m, jnp.max(s, axis=0, keepdims=True))
        l = jnp.zeros((1, 256), F32)
        dl = jnp.zeros((1, 256), F32)
        for j in range(nk):
            rows = pl.ds(j * CK, CK)
            e = jnp.exp2((s_ref[rows, :] - m) * EXPC)
            dp = dot_nt(kv_ref[rows, 128:256], g)
            l = l + jnp.sum(e, axis=0, keepdims=True)
            dl = dl + jnp.sum(e * dp, axis=0, keepdims=True)
            s_ref[rows, :] = e
            d_ref[rows, :] = dp
        inv = 1.0 / l
        delta = dl * inv
        if variant == "kt":
            dq = jnp.zeros((128, 256), F32)
        else:
            dq = jnp.zeros((256, 128), F32)
        for j in range(nk):
            rows = pl.ds(j * CK, CK)
            p = s_ref[rows, :] * inv
            ds = (p * (d_ref[rows, :] - delta)).astype(BF16)
            dk_ref[rows, :] += dot_nn(ds, q)
            dv_ref[rows, :] += dot_nn(p.astype(BF16), g)
            if variant == "kt":
                dq = dq + dot_nn(kt_ref[:, j * CK:(j + 1) * CK], ds)
            else:
                dq = dq + dot_tn(ds, kv_ref[rows, 0:128])
        if variant == "kt":
            dq = dq.T
        dq_ref[yl, :, cols] = (dq * SCALE).astype(BF16)

    def head(h, carry):
        unit(h, 0, 6)
        unit(h, 1, 7)
        return carry

    lax.fori_loop(0, 4, head, 0)
    for j in range(7):
        rows = pl.ds(j * CK, CK)
        kvg_ref[rows, 0:128] = (dk_ref[rows, :] * SCALE).astype(BF16)
        kvg_ref[rows, 128:256] = dv_ref[rows, :].astype(BF16)
    kvg_ref[pl.ds(3584, CK), :] = jnp.zeros((CK, 256), BF16)


def attention(q, g, kv, lim, variant="tn"):
    return pl.pallas_call(
        functools.partial(att_body, variant=variant),
        name="attention_grads",
        out_shape=(jax.ShapeDtypeStruct((2, 256, 512), BF16), jax.ShapeDtypeStruct((4096, 256), BF16)),
        in_specs=[pl.BlockSpec(memory_space=pltpu.VMEM)] * 4,
        out_specs=[pl.BlockSpec(memory_space=pltpu.VMEM)] * 2,
        scratch_shapes=[
            pltpu.VMEM((3584, 256), F32),
            pltpu.VMEM((3584, 256), F32),
            pltpu.VMEM((3584, 128), F32),
            pltpu.VMEM((3584, 128), F32),
            pltpu.VMEM((128, 3584), BF16),
        ],
        compiler_params=pltpu.CompilerParams(vmem_limit_bytes=56 << 20),
    )(q, g, kv, lim)


def coords():
    seq = lax.axis_index("seq")
    c = lax.rem(seq, 2)
    x = lax.rem(seq // 2, 4)
    zh = lax.rem(seq // 8, 2)
    yl = lax.rem(seq // 16, 2)
    s = seq // 32
    zl = lax.axis_index("dp")
    return s, yl, zh, x, c, zl


def seq_of(s, yl, zh, x, c):
    return s * 32 + yl * 16 + zh * 8 + x * 2 + c


def rcopy(src, dst, ssem, rsem, seq, dp):
    return pltpu.make_async_remote_copy(
        src_ref=src, dst_ref=dst, send_sem=ssem, recv_sem=rsem,
        device_id={"seq": seq, "dp": dp}, device_id_type=pl.DeviceIdType.MESH)


def greet(peers):
    barrier = pltpu.get_barrier_semaphore()
    for seq, dp in peers:
        pl.semaphore_signal(barrier, inc=1, device_id={"seq": seq, "dp": dp},
                            device_id_type=pl.DeviceIdType.MESH)
    pl.semaphore_wait(barrier, len(peers))


def gather_body(q_in, g_in, k_in, v_in, q_out, g_out, kv_out,
                g_send, g_recv, z_send, z_recv, x_send, x_recv, l_sem):
    s, yl, zh, x, c, zl = coords()
    group = []
    for d in range(1, 4):
        dy, dc = d // 2, d % 2
        group.append(((yl + dy) % 2, (c + dc) % 2))
    xs = [(x + d) % 4 for d in range(1, 4)]
    peers = [(seq_of(s, py, zh, x, pc), zl) for py, pc in group]
    peers.append((seq_of(s, yl, 1 - zh, x, c), zl))
    peers += [(seq_of(s, yl, zh, px, c), zl) for px in xs]
    greet(peers)

    def cols(h, w):
        return pl.ds(pl.multiple_of(h * w, 128), w)

    my_rows = pl.ds(pl.multiple_of(c * 128, 128), 128)
    kv_sends = []
    sends = []
    for i, (py, pc) in enumerate(group):
        h = py * 2 + pc
        dev = seq_of(s, py, zh, x, pc)
        kv_sends.append(rcopy(k_in.at[0, :, cols(h, 128)], kv_out.at[yl, zh, x, my_rows, pl.ds(0, 128)],
                              g_send.at[0, i], g_recv.at[0, i], dev, zl))
        kv_sends.append(rcopy(v_in.at[0, :, cols(h, 128)], kv_out.at[yl, zh, x, my_rows, pl.ds(128, 128)],
                              g_send.at[1, i], g_recv.at[1, i], dev, zl))
    for i, (py, pc) in enumerate(group):
        h = py * 2 + pc
        dev = seq_of(s, py, zh, x, pc)
        sends.append(rcopy(q_in.at[0, :, cols(h, 512)], q_out.at[yl, my_rows, :],
                           g_send.at[2, i], g_recv.at[2, i], dev, zl))
        sends.append(rcopy(g_in.at[0, :, cols(h, 512)], g_out.at[yl, my_rows, :],
                           g_send.at[3, i], g_recv.at[3, i], dev, zl))
    for cp in kv_sends:
        cp.start()
    h = yl * 2 + c
    own_kv = [
        pltpu.make_async_copy(k_in.at[0, :, cols(h, 128)], kv_out.at[yl, zh, x, my_rows, pl.ds(0, 128)], l_sem.at[0]),
        pltpu.make_async_copy(v_in.at[0, :, cols(h, 128)], kv_out.at[yl, zh, x, my_rows, pl.ds(128, 128)], l_sem.at[1]),
    ]
    own = [
        pltpu.make_async_copy(q_in.at[0, :, cols(h, 512)], q_out.at[yl, my_rows, :], l_sem.at[2]),
        pltpu.make_async_copy(g_in.at[0, :, cols(h, 512)], g_out.at[yl, my_rows, :], l_sem.at[3]),
    ]
    for cp in own_kv + own:
        cp.start()
    for cp in sends:
        cp.start()
    for cp in own_kv:
        cp.wait()
    for cp in kv_sends:
        cp.wait_recv()
    zcopy = rcopy(kv_out.at[:, zh, x], kv_out.at[:, zh, x], z_send, z_recv,
                  seq_of(s, yl, 1 - zh, x, c), zl)
    zcopy.start()
    xcopies = []
    for i, px in enumerate(xs):
        cp = rcopy(kv_out.at[:, zh, x], kv_out.at[:, zh, x], x_send.at[0, i], x_recv.at[0, i],
                   seq_of(s, yl, zh, px, c), zl)
        cp.start()
        xcopies.append(cp)
    zcopy.wait_recv()
    for i, px in enumerate(xs):
        cp = rcopy(kv_out.at[:, 1 - zh, x], kv_out.at[:, 1 - zh, x], x_send.at[1, i], x_recv.at[1, i],
                   seq_of(s, yl, zh, px, c), zl)
        cp.start()
        xcopies.append(cp)
    for cp in own:
        cp.wait()
    for cp in sends:
        cp.wait_recv()
    for cp in xcopies:
        cp.wait_recv()
    for cp in kv_sends + sends + [zcopy] + xcopies:
        cp.wait_send()


def gather(q, g, k, v):
    dma = pltpu.SemaphoreType.DMA
    return pl.pallas_call(
        gather_body,
        name="gather_heads",
        out_shape=(jax.ShapeDtypeStruct((2, 256, 512), BF16), jax.ShapeDtypeStruct((2, 256, 512), BF16),
                   jax.ShapeDtypeStruct((2, 2, 4, 256, 256), BF16)),
        in_specs=[pl.BlockSpec(memory_space=pl.ANY)] * 4,
        out_specs=[pl.BlockSpec(memory_space=pl.ANY)] * 3,
        scratch_shapes=[dma((4, 3)), dma((4, 3)), dma, dma, dma((2, 3)), dma((2, 3)), dma((4,))],
        compiler_params=pltpu.CompilerParams(collective_id=0, has_side_effects=True),
    )(q, g, k, v)


def reduce_body(dq_in, kvg_in, n_in, dq_out, kg_out, vg_out, w_out,
                nbuf, xr, acc, zsend, zrecv, kg, wpart, w1r, w2r, w2s, w3r, w3s, w4s, w4r,
                n_send, n_recv, q_send, q_recv, x_send, x_recv, z_send, z_recv, k_send, k_recv,
                w1_send, w1_recv, w2_send, w2_recv, w3_send, w3_recv, w4_send, w4_recv, l_sem):
    s, yl, zh, x, c, zl = coords()
    me = seq_of(s, yl, zh, x, c)
    group = []
    for d in range(1, 4):
        dy, dc = d // 2, d % 2
        group.append(((yl + dy) % 2, (c + dc) % 2))
    xs = [(x + d) % 4 for d in range(1, 4)]
    z = zh * 4 + zl
    zs = [((z + d) % 8) for d in range(1, 8)]
    peers = [(seq_of(s, py, zh, x, pc), zl) for py, pc in group]
    peers += [(seq_of(s, yl, zh, px, c), zl) for px in xs]
    peers += [(seq_of(s, yl, pz // 4, x, c), pz % 4) for pz in zs]
    peers.append((seq_of(1 - s, yl, zh, x, c), zl))
    greet(peers)

    def cols(h, w):
        return pl.ds(pl.multiple_of(h * w, 128), w)

    h = yl * 2 + c
    my_rows = pl.ds(pl.multiple_of(c * 128, 128), 128)
    sends = []

    def go(cp):
        cp.start()
        sends.append(cp)
        return cp

    far = [go(rcopy(kvg_in.at[:, 1 - zh, px], xr.at[0, i], x_send.at[0, i], x_recv.at[0, i],
                    seq_of(s, yl, zh, px, c), zl)) for i, px in enumerate(xs)]
    near = [go(rcopy(kvg_in.at[:, zh, px], xr.at[1, i], x_send.at[1, i], x_recv.at[1, i],
                     seq_of(s, yl, zh, px, c), zl)) for i, px in enumerate(xs)]
    own_a = pltpu.make_async_copy(kvg_in.at[:, 1 - zh, x], zsend, l_sem.at[0])
    own_b = pltpu.make_async_copy(kvg_in.at[:, zh, x], kg, l_sem.at[1])
    own_a.start()
    own_b.start()
    n_own = pltpu.make_async_copy(n_in.at[0], nbuf.at[yl, my_rows, :], l_sem.at[2])
    n_own.start()
    n_y = go(rcopy(n_in.at[0], nbuf.at[yl, my_rows, :], n_send.at[0], n_recv.at[0],
                   seq_of(s, 1 - yl, zh, x, c), zl))
    n_c = go(rcopy(n_in.at[0], nbuf.at[yl, my_rows, :], n_send.at[1], n_recv.at[1],
                   seq_of(s, yl, zh, x, 1 - c), zl))
    dq_own = pltpu.make_async_copy(dq_in.at[yl, my_rows, :], dq_out.at[0, :, cols(h, 512)], l_sem.at[3])
    dq_own.start()
    dqs = []
    for i, (py, pc) in enumerate(group):
        dqs.append(go(rcopy(dq_in.at[py, pl.ds(pl.multiple_of(pc * 128, 128), 128), :],
                            dq_out.at[0, :, cols(h, 512)], q_send.at[i], q_recv.at[i],
                            seq_of(s, py, zh, x, pc), zl)))
    own_a.wait()
    for cp in far:
        cp.wait_recv()
    zsend[...] = (zsend[...].astype(F32) + xr[0, 0].astype(F32) + xr[0, 1].astype(F32)
                  + xr[0, 2].astype(F32)).astype(BF16)
    zc = go(rcopy(zsend, zrecv, z_send, z_recv, seq_of(s, yl, 1 - zh, x, c), zl))
    own_b.wait()
    for cp in near:
        cp.wait_recv()
    acc[...] = (kg[...].astype(F32) + xr[1, 0].astype(F32) + xr[1, 1].astype(F32) + xr[1, 2].astype(F32))
    n_y.wait_recv()
    other = nbuf.at[1 - yl, my_rows, :]
    n_f = go(rcopy(other, other, n_send.at[2], n_recv.at[2], seq_of(s, yl, zh, x, 1 - c), zl))
    zc.wait_recv()
    kg[...] = (acc[...] + zrecv[...].astype(F32)).astype(BF16)
    kgs = []
    for i, (py, pc) in enumerate(group):
        prow = pl.ds(pl.multiple_of(pc * 128, 128), 128)
        dev = seq_of(s, py, zh, x, pc)
        kgs.append(go(rcopy(kg.at[py, prow, pl.ds(0, 128)], kg_out.at[0, :, cols(h, 128)],
                            k_send.at[0, i], k_recv.at[0, i], dev, zl)))
        kgs.append(go(rcopy(kg.at[py, prow, pl.ds(128, 128)], vg_out.at[0, :, cols(h, 128)],
                            k_send.at[1, i], k_recv.at[1, i], dev, zl)))
    k_own = [pltpu.make_async_copy(kg.at[yl, my_rows, pl.ds(0, 128)], kg_out.at[0, :, cols(h, 128)], l_sem.at[4]),
             pltpu.make_async_copy(kg.at[yl, my_rows, pl.ds(128, 128)], vg_out.at[0, :, cols(h, 128)], l_sem.at[5])]
    for cp in k_own:
        cp.start()
    n_own.wait()
    n_c.wait_recv()
    n_f.wait_recv()
    kgv = kg[...].reshape(512, 256)

    def wblock(i, carry):
        rows = pl.ds(pl.multiple_of(i * 512, 512), 512)
        part = dot_tn(nbuf[:, :, rows].reshape(512, 512), kgv)
        wpart[pl.ds(i, 1)] = part.astype(BF16).reshape(1, 4, 128, 256)
        return carry

    lax.fori_loop(0, 8, wblock, 0)
    w1 = [go(rcopy(wpart.at[:, px], w1r.at[i], w1_send.at[i], w1_recv.at[i],
                   seq_of(s, yl, zh, px, c), zl)) for i, px in enumerate(xs)]
    for cp in w1:
        cp.wait_recv()

    def add1(i, carry):
        blk = pl.ds(i, 1)
        a = wpart[blk, pl.ds(x, 1)].reshape(128, 256).astype(F32)
        a = a + w1r[0, blk].reshape(128, 256).astype(F32) + w1r[1, blk].reshape(128, 256).astype(F32)
        a = a + w1r[2, blk].reshape(128, 256).astype(F32)
        w2s[pl.ds(i // 2, 1), pl.ds(lax.rem(i, 2), 1)] = a.astype(BF16).reshape(1, 1, 2, 4, 16, 256)
        return carry

    lax.fori_loop(0, 8, add1, 0)
    w2 = [go(rcopy(w2s.at[:, pz // 4, :, pz % 4], w2r.at[i], w2_send.at[i], w2_recv.at[i],
                   seq_of(s, yl, pz // 4, x, c), pz % 4)) for i, pz in enumerate(zs)]
    for cp in w2:
        cp.wait_recv()
    t = w2s[:, pl.ds(zh, 1), :, pl.ds(zl, 1)].reshape(4, 2, 16, 256).astype(F32)
    for i in range(7):
        t = t + w2r[i].astype(F32)
    w3s[...] = t.reshape(2, 2, 2, 16, 256)
    w3 = go(rcopy(w3s.at[1 - s], w3r, w3_send, w3_recv, seq_of(1 - s, yl, zh, x, c), zl))
    w3.wait_recv()
    w4s[...] = w3s[s] + w3r[...]
    w4 = []
    for i, (py, pc) in enumerate(group):
        w4.append(go(rcopy(w4s.at[py, pc], w4r.at[h], w4_send.at[i], w4_recv.at[i],
                           seq_of(s, py, zh, x, pc), zl)))
    w4r[pl.ds(h, 1)] = w4s[yl, c].reshape(1, 16, 256)
    for cp in w4:
        cp.wait_recv()
    for hh in range(4):
        w_out[:, hh * 128:(hh + 1) * 128] = w4r[hh, :, 0:128]
        w_out[:, 512 + hh * 128:512 + (hh + 1) * 128] = w4r[hh, :, 128:256]
    for cp in dqs + kgs:
        cp.wait_recv()
    for cp in k_own + [dq_own]:
        cp.wait()
    for cp in sends:
        cp.wait_send()


def reduce_all(dq, kvg, n):
    dma = pltpu.SemaphoreType.DMA
    V = pltpu.VMEM
    return pl.pallas_call(
        reduce_body,
        name="reduce_grads",
        out_shape=(jax.ShapeDtypeStruct((1, 128, 2048), BF16), jax.ShapeDtypeStruct((1, 128, 512), BF16),
                   jax.ShapeDtypeStruct((1, 128, 512), BF16), jax.ShapeDtypeStruct((16, 1024), F32)),
        in_specs=[pl.BlockSpec(memory_space=pl.ANY)] * 3,
        out_specs=[pl.BlockSpec(memory_space=pl.ANY)] * 3 + [pl.BlockSpec(memory_space=pltpu.VMEM)],
        scratch_shapes=[
            V((2, 256, 4096), BF16), V((2, 3, 2, 256, 256), BF16), V((2, 256, 256), F32),
            V((2, 256, 256), BF16), V((2, 256, 256), BF16), V((2, 256, 256), BF16),
            V((8, 4, 128, 256), BF16), V((3, 8, 128, 256), BF16),
            V((7, 4, 2, 16, 256), BF16), V((4, 2, 2, 4, 16, 256), BF16),
            V((2, 2, 16, 256), F32), V((2, 2, 2, 16, 256), F32),
            V((2, 2, 16, 256), F32), V((4, 16, 256), F32),
            dma((3,)), dma((3,)), dma((3,)), dma((3,)), dma((2, 3)), dma((2, 3)), dma, dma,
            dma((2, 3)), dma((2, 3)), dma((3,)), dma((3,)), dma((7,)), dma((7,)), dma, dma, dma((3,)), dma((3,)),
            dma((6,)),
        ],
        compiler_params=pltpu.CompilerParams(collective_id=1, has_side_effects=True, vmem_limit_bytes=48 << 20),
    )(dq, kvg, n)


def local(query, keys, values, out_grad, normed_input, q_start, q_len):
    s, yl, zh, x, c, zl = coords()
    start = lax.dynamic_index_in_dim(q_start, s, 0, keepdims=False)
    end = start + lax.dynamic_index_in_dim(q_len, s, 0, keepdims=False)
    pos = (jnp.arange(2, dtype=jnp.int32)[:, None, None] * 2048 + zh * 1024 + x * 256
           + jnp.arange(256, dtype=jnp.int32)[None, None, :])
    lim = jnp.maximum(start, jnp.minimum(end, pos + 1))
    q_rx, g_rx, kv = gather(query, out_grad, keys, values)
    dq, kvg = attention(q_rx, g_rx, kv.reshape(4096, 256), lim)
    return reduce_all(dq, kvg.reshape(2, 2, 4, 256, 256), normed_input)


def solution(mesh):
    tok = P("dp", "seq", None)
    return jax.shard_map(
        local, mesh=mesh,
        in_specs=(tok, tok, tok, tok, tok, P("dp"), P("dp")),
        out_specs=(tok, tok, tok, P(("seq", "dp"), None)),
        check_vma=False)
```

time: 1880 us -> 168 us (0.09)
  waiting for transfers between devices: 1470 us -> 0 us
  Pallas kernels: 0 us -> 157 us
  local copies, waits for them, and re-layouts: 120 us -> 7.85 us
  matrix products: 109 us -> 0 us
  starting transfers between devices: 65.9 us -> 0 us
  other arithmetic: 66.8 us -> 1.31 us
    unnamed x2 -> x0, waiting for transfers between devices: 1270 us -> none
    all_to_all x6 -> x0, waiting for transfers between devices: 209 us -> none  [the longest x1 51 us: local(): lax.all_to_all(key_units, 'seq', split_axis=1, concat_axis=0, tiled=True)]
    pallas_call x0 -> x3, Pallas kernels: none -> 157 us  [the longest x1 84.7 us: reduce_all(): pl.pallas_call(reduce_body, name='reduce_grads', out_shape=(jax.ShapeDtyp...]
    dot_general x21 -> x0, matrix products: 109 us -> none  [the longest x4 37.7 us: one_block(): jnp.einsum('qhd,khd->hqk', grad_block, value_block, preferred_element_typ...]
    all_to_all x6 -> x0, starting transfers between devices: 65.9 us -> none  [the longest x1 25.4 us: local(): lax.all_to_all(value_acc.reshape(seq_count, tokens_dev, 1, width_dev).ast...]
    convert_element_type x6 -> x0, other arithmetic: 44.8 us -> none  [the longest x4 40.1 us: one_block(): (probability * (dprob - row_delta) * score_scale).astype(jnp.bfloat16)]
    dynamic_update_slice x20 -> x0, local copies, waits for them, and re-layouts: 39.1 us -> none  [the longest x8 28.5 us: one_block(): lax.dynamic_update_slice_in_dim(value_acc, value_part, key_first, 0)]
    dynamic_slice x24 -> x2, local copies, waits for them, and re-layouts: 39.3 us -> 2.48 us  [the longest x1 1.24 us: local(): end = start + lax.dynamic_index_in_dim(q_len, s, 0, keepdims=False)]
  transfers between devices with their start and end apart: 7 -> 0, of which waited for: 7 -> 0; matrix products, arithmetic and copies ran while one was open for 1% -> 0% of each run, Pallas kernels for 0% -> 0%
where the time goes in v1:
time: 168 us
  Pallas kernels  157 us (93%)
  local copies, waits for them, and re-layouts  7.85 us (5%)
  between operations  2 us (1%)
    pallas_call x1, Pallas kernels, reduce_all(): pl.pallas_call(reduce_body, name='reduce_grads', out_shape=(jax.ShapeDtyp...  84.7 us
    pallas_call x1, Pallas kernels, gather(): pl.pallas_call(gather_body, name='gather_heads', out_shape=(jax.ShapeDtyp...  40.6 us
    pallas_call x1, Pallas kernels, attention(): pl.pallas_call(functools.partial(att_body, variant=variant), name='attent...  31.7 us
    unnamed x10, local copies, waits for them, and re-layouts  5.37 us

profile of v1, /device:TPU:1, one launch (start us, length us, event | category | flops | bytes accessed | tf_op | source)
XLA Modules:
  0.0 168.2 jit_solution(17099407719673368427)
XLA Ops:
  0.7 1.2 dynamic_slice.8
  1.9 1.2 dynamic_slice.7
  4.5 1.3 minimum_maximum_fusion.lim_ref
  5.8 0.0 copy-start.1
  5.8 40.6 %gather_heads.1 = (bf16[2,256,512]{2,1,0:T(8,128)(2,1)}, bf16[2,256,512]{2,1,0:T(8,128)(2,1)}, bf16[2,2,4,256,256]{4,3,2,1,0:T(8,128)(2,1)}) custom-call(bf16[1,128,2048]{2,1,0:T(8,128)(2,1)} %q_in.1, bf16[1,128,2048]{2,1,0:T(8,128)(2,1)} %g_in.1, bf16[1,128,512]{2,1,0:T(8,128)(2,1)} %k_in.1, bf16[1,128,512]{2,1,0:T(8,128)(2,1)} %v_in.1), custom_call_target="tpu_custom_call" | custom-call | tf_op jit(solution)/shard_map/gather_heads/pallas_call | solution.py:221
  46.4 31.7 %attention_grads.1 = (bf16[2,256,512]{2,1,0:T(8,128)(2,1)}, bf16[4096,256]{1,0:T(8,128)(2,1)}) custom-call(bf16[2,256,512]{2,1,0:T(8,128)(2,1)} %get-tuple-element.9.q_ref, bf16[2,256,512]{2,1,0:T(8,128)(2,1)} %get-tuple-element.10.g_ref, bf16[4096,256]{1,0:T(8,128)(2,1)} %bitcast.5, s32[2,1,256]{2,1,0:T(1,128)} %minimum_maximum_fusion.lim_ref), custom_call_target="tpu_custom_call" | custom-call | tf_op jit(solution)/shard_map/attention_grads/pallas_call | solution.py:96
  78.1 0.0 copy-done.1
  78.2 0.0 copy-start
  78.2 1.6 copy-done
  79.7 0.0 copy-start.2
  79.7 1.0 copy-done.2
  80.8 84.7 %reduce_grads.1 = (bf16[1,128,2048]{2,1,0:T(8,128)(2,1)S(1)}, bf16[1,128,512]{2,1,0:T(8,128)(2,1)S(1)}, bf16[1,128,512]{2,1,0:T(8,128)(2,1)S(1)}, f32[16,1024]{1,0:T(8,128)S(1)}) custom-call(bf16[2,256,512]{2,1,0:T(8,128)(2,1)S(1)} %copy-done.2, bf16[2,2,4,256,256]{4,3,2,1,0:T(8,128)(2,1)S(1)} %bitcast.4, bf16[1,128,4096]{2,1,0:T(8,128)(2,1)S(1)} %copy-done.1), custom_call_target="tpu_custom_call" | custom-call | tf_op jit(solution)/shard_map/reduce_grads/pallas_call | solution.py:370
  165.5 0.8 copy.15
  166.3 0.7 copy.16
  167.0 0.7 copy.17
  167.6 0.6 copy.18
  (1 shorter events, 0.0 us)
Async XLA Ops:
  5.8 72.4 %copy-start.1 = (bf16[1,128,4096]{2,1,0:T(8,128)(2,1)S(1)}, bf16[1,128,4096]{2,1,0:T(8,128)(2,1)}, u32[]{:S(2)}) copy-start(bf16[1,128,4096]{2,1,0:T(8,128)(2,1)} %n_in.1) | copy-start | bytes 3145732
  78.2 1.6 copy-start
  79.7 1.0 copy-start.2

commit v2 on v0

v2 whole, which is shorter than its diff:
```python
import math
import jax
import jax.numpy as jnp
from jax import lax
from jax.experimental import pallas as pl
from jax.experimental.pallas import tpu as pltpu
from jax.sharding import PartitionSpec as P

HEAD_DIM = 128
SCALE = 1.0 / math.sqrt(HEAD_DIM)
EXPC = SCALE * math.log2(math.e)
NEG = -1e30
F32 = jnp.float32
BF16 = jnp.bfloat16
CK = 512


def dot_nt(a, b):
    return lax.dot_general(a, b, (((1,), (1,)), ((), ())), preferred_element_type=F32)


def dot_nn(a, b):
    return lax.dot_general(a, b, (((1,), (0,)), ((), ())), preferred_element_type=F32)


def dot_tn(a, b):
    return lax.dot_general(a, b, (((0,), (0,)), ((), ())), preferred_element_type=F32)


def coords():
    seq = lax.axis_index("seq")
    c = lax.rem(seq, 2)
    x = lax.rem(seq // 2, 4)
    zh = lax.rem(seq // 8, 2)
    yl = lax.rem(seq // 16, 2)
    s = seq // 32
    zl = lax.axis_index("dp")
    return s, yl, zh, x, c, zl


def seq_of(s, yl, zh, x, c):
    return s * 32 + yl * 16 + zh * 8 + x * 2 + c


def rcopy(src, dst, ssem, rsem, dev):
    return pltpu.make_async_remote_copy(
        src_ref=src, dst_ref=dst, send_sem=ssem, recv_sem=rsem,
        device_id={"seq": dev[0], "dp": dev[1]}, device_id_type=pl.DeviceIdType.MESH)


def greet(peers):
    barrier = pltpu.get_barrier_semaphore()
    for seq, dp in peers:
        pl.semaphore_signal(barrier, inc=1, device_id={"seq": seq, "dp": dp},
                            device_id_type=pl.DeviceIdType.MESH)
    pl.semaphore_wait(barrier, len(peers))


def blk(i, w):
    return pl.ds(pl.multiple_of(i * w, w), w)


def body(q_in, g_in, k_in, v_in, n_in, start_ref, len_ref,
         dq_out, kg_out, vg_out, w_out,
         q_ref, g_ref, kv, nbuf, s_ref, d_ref, dk_ref, dv_ref, dq_ref,
         csend, crx, ysend, yrx, acc0, acc1, zsend, zrx, kga,
         w1s, w1r, w2s, w2r, w3s, w4r,
         kx_s, kx_r, qx_s, qx_r, kz_s, kz_r, ky_s, ky_r, kc_s, kc_r, n_s, n_r, dq_s, dq_r,
         c_s, c_r, y_s, y_r, z_s, z_r, kc2_s, kc2_r, ko_s, ko_r,
         w1_s, w1_r, w2_s, w2_r, w4_s, w4_r, l_sem, nl_sem, dql_sem):
    s, yl, zh, x, c, zl = coords()
    y = s * 2 + yl
    z = zh * 4 + zl
    me8 = x * 2 + c

    def dev(s_=None, yl_=None, zh_=None, x_=None, c_=None, zl_=None):
        return (seq_of(s if s_ is None else s_, yl if yl_ is None else yl_, zh if zh_ is None else zh_,
                       x if x_ is None else x_, c if c_ is None else c_), zl if zl_ is None else zl_)

    row8 = [lax.rem(me8 + d, 8) for d in range(1, 8)]
    xs = [lax.rem(x + d, 4) for d in range(1, 4)]
    ys = [lax.rem(y + d, 4) for d in range(1, 4)]
    zs = [lax.rem(z + d, 8) for d in range(1, 8)]
    ydev = [dev(s_=p // 2, yl_=lax.rem(p, 2)) for p in ys]
    zdev = [dev(zh_=p // 4, zl_=lax.rem(p, 4)) for p in zs]
    core_dev = dev(c_=1 - c)
    y_dev = dev(yl_=1 - yl)
    z_dev = dev(zh_=1 - zh)
    greet([dev(x_=p // 2, c_=lax.rem(p, 2)) for p in row8] + ydev + zdev)

    sends = []

    def go(cp):
        cp.start()
        sends.append(cp)
        return cp

    crow = blk(c, 128)
    orow = blk(1 - c, 128)

    kx = []
    for i, px in enumerate(xs):
        kx.append((go(rcopy(k_in.at[0, :, blk(px, 128)], kv.at[yl, zh, x, crow, pl.ds(0, 128)],
                            kx_s.at[0, i], kx_r.at[0, i], dev(x_=px))),
                   go(rcopy(v_in.at[0, :, blk(px, 128)], kv.at[yl, zh, x, crow, pl.ds(128, 128)],
                            kx_s.at[1, i], kx_r.at[1, i], dev(x_=px)))))
    own_kv = [pltpu.make_async_copy(k_in.at[0, :, blk(x, 128)], kv.at[yl, zh, x, crow, pl.ds(0, 128)], l_sem.at[0]),
              pltpu.make_async_copy(v_in.at[0, :, blk(x, 128)], kv.at[yl, zh, x, crow, pl.ds(128, 128)], l_sem.at[1])]
    own_q = [pltpu.make_async_copy(q_in.at[0, :, blk(x, 512)], q_ref.at[x], l_sem.at[2]),
             pltpu.make_async_copy(g_in.at[0, :, blk(x, 512)], g_ref.at[x], l_sem.at[3])]
    for cp in own_kv + own_q:
        cp.start()
    qx = []
    for i, px in enumerate(xs):
        qx.append(go(rcopy(q_in.at[0, :, blk(px, 512)], q_ref.at[x], qx_s.at[0, i], qx_r.at[0, i], dev(x_=px))))
        qx.append(go(rcopy(g_in.at[0, :, blk(px, 512)], g_ref.at[x], qx_s.at[1, i], qx_r.at[1, i], dev(x_=px))))

    def piece(yl_, zh_, k):
        return kv.at[yl_, zh_, lax.rem(x - k + 4, 4), crow]

    zc, y0, y1, cc = [], [], [], []
    for k in range(4):
        for cp in (own_kv if k == 0 else ()):
            cp.wait()
        if k:
            kx[k - 1][0].wait_recv()
            kx[k - 1][1].wait_recv()
        p = piece(yl, zh, k)
        zc.append(go(rcopy(p, p, kz_s.at[k], kz_r.at[k], z_dev)))
        y0.append(go(rcopy(p, p, ky_s.at[0, k], ky_r.at[0, k], y_dev)))
        cc.append(go(rcopy(p, p, kc_s.at[0, k], kc_r.at[0, k], core_dev)))
    for k in range(4):
        y0[k].wait_recv()
        p = piece(1 - yl, zh, k)
        cc.append(go(rcopy(p, p, kc_s.at[1, k], kc_r.at[1, k], core_dev)))
    for k in range(4):
        zc[k].wait_recv()
        p = piece(yl, 1 - zh, k)
        y1.append(go(rcopy(p, p, ky_s.at[1, k], ky_r.at[1, k], y_dev)))
        cc.append(go(rcopy(p, p, kc_s.at[2, k], kc_r.at[2, k], core_dev)))
    for cp in own_q:
        cp.wait()
    for cp in qx:
        cp.wait_recv()

    def nsend(rr, carry):
        for i, t in enumerate(row8):
            tc = lax.rem(t, 2)
            rcopy(n_in.at[0, :, pl.ds(pl.multiple_of(rr * 512 + tc * 256, 256), 256)], nbuf.at[rr, x, c],
                  n_s.at[i, rr], n_r.at[i, rr], dev(x_=t // 2, c_=tc)).start()
        pltpu.make_async_copy(n_in.at[0, :, pl.ds(pl.multiple_of(rr * 512 + c * 256, 256), 256)],
                              nbuf.at[rr, x, c], nl_sem.at[rr]).start()
        return carry

    lax.fori_loop(0, 8, nsend, 0)

    for k in range(4):
        y1[k].wait_recv()
        p = piece(1 - yl, 1 - zh, k)
        cc.append(go(rcopy(p, p, kc_s.at[3, k], kc_r.at[3, k], core_dev)))
    for cp in cc:
        cp.wait_recv()

    start = start_ref[s]
    end = start + len_ref[s]
    dk_ref[...] = jnp.zeros_like(dk_ref)
    dv_ref[...] = jnp.zeros_like(dv_ref)
    lane = lax.broadcasted_iota(jnp.int32, (1, 256), 1)

    def keys(j):
        return kv[j // 4, (j // 2) % 2, (j % 2) * 2:(j % 2) * 2 + 2, :, 0:128].reshape(CK, 128)

    def values(j):
        return kv[j // 4, (j // 2) % 2, (j % 2) * 2:(j % 2) * 2 + 2, :, 128:256].reshape(CK, 128)

    def unit(h, half, nk):
        cols = blk(h, 128)
        q = q_ref[2 * half:2 * half + 2, :, cols].reshape(256, 128)
        g = g_ref[2 * half:2 * half + 2, :, cols].reshape(256, 128)
        pos = yl * 2048 + zh * 1024 + (2 * half + lane // 128) * 256 + c * 128 + lax.rem(lane, 128)
        lim = jnp.maximum(start, jnp.minimum(end, pos + 1))
        m = jnp.full((1, 256), NEG, F32)
        for j in range(nk):
            rows = pl.ds(j * CK, CK)
            sc = dot_nt(keys(j), q)
            if j >= 4:
                kpos = lax.broadcasted_iota(jnp.int32, (CK, 256), 0) + j * CK
                sc = jnp.where(kpos < lim, sc, NEG)
            s_ref[rows, :] = sc
            m = jnp.maximum(m, jnp.max(sc, axis=0, keepdims=True))
        l = jnp.zeros((1, 256), F32)
        dl = jnp.zeros((1, 256), F32)
        for j in range(nk):
            rows = pl.ds(j * CK, CK)
            e = jnp.exp2((s_ref[rows, :] - m) * EXPC)
            dp = dot_nt(values(j), g)
            l = l + jnp.sum(e, axis=0, keepdims=True)
            dl = dl + jnp.sum(e * dp, axis=0, keepdims=True)
            s_ref[rows, :] = e
            d_ref[rows, :] = dp
        inv = 1.0 / l
        delta = dl * inv
        dq = jnp.zeros((256, 128), F32)
        for j in range(nk):
            rows = pl.ds(j * CK, CK)
            p = s_ref[rows, :] * inv
            ds = (p * (d_ref[rows, :] - delta)).astype(BF16)
            dk_ref[rows, :] += dot_nn(ds, q)
            dv_ref[rows, :] += dot_nn(p.astype(BF16), g)
            dq = dq + dot_tn(ds, keys(j))
        dq_ref[2 * half:2 * half + 2, :, cols] = (dq * SCALE).astype(BF16).reshape(2, 128, 128)

    def dq_copy(h, i):
        px = xs[i]
        return rcopy(dq_ref.at[px, :, blk(h, 128)], dq_out.at[0, :, blk(x * 4 + h, 128)],
                     dq_s.at[h, i], dq_r.at[h, i], dev(x_=px))

    def dq_local(h):
        return pltpu.make_async_copy(dq_ref.at[x, :, blk(h, 128)], dq_out.at[0, :, blk(x * 4 + h, 128)],
                                     dql_sem.at[h])

    def heads(nk):
        def head(h, carry):
            unit(h, 0, nk)
            unit(h, 1, nk)
            for i in range(3):
                dq_copy(h, i).start()
            dq_local(h).start()
            return carry
        lax.fori_loop(0, 4, head, 0)

    last = yl * zh

    @pl.when(last == 1)
    def _():
        heads(7)

    @pl.when(last == 0)
    def _():
        heads(6)

    def grads(yl_, zh_, x_, c_):
        r = pl.ds(pl.multiple_of(((yl_ * 2 + zh_) * 4 + x_) * 256 + c_ * 128, 128), 128)
        return jnp.concatenate([dk_ref[r, :] * SCALE, dv_ref[r, :]], axis=1)

    quad = [(1 - yl, 1 - zh), (yl, 1 - zh), (1 - yl, zh), (yl, zh)]
    cx = []
    for k, (a, b) in enumerate(quad):
        for x_ in range(4):
            csend[k, x_] = grads(a, b, x_, 1 - c).astype(BF16)
        cx.append(go(rcopy(csend.at[k], crx.at[k], c_s.at[k], c_r.at[k], core_dev)))

    def pair(k, x_):
        a, b = quad[k]
        return grads(a, b, x_, c) + crx[k, x_].astype(F32)

    yx = {}

    def y_stage(k, slot):
        cx[k].wait_recv()
        for hp in range(2):
            for x_ in (2 * hp, 2 * hp + 1):
                ysend[slot, x_] = pair(k, x_).astype(BF16)
            part = pl.ds(2 * hp, 2)
            yx[slot, hp] = go(rcopy(ysend.at[slot, part], yrx.at[slot, part], y_s.at[slot, hp], y_r.at[slot, hp], y_dev))

    y_stage(0, 0)
    cx[1].wait_recv()
    for x_ in range(4):
        acc1[x_] = pair(1, x_)
    y_stage(2, 1)
    cx[3].wait_recv()
    for x_ in range(4):
        acc0[x_] = pair(3, x_)
    zx = []
    for hp in range(2):
        yx[0, hp].wait_recv()
        part = pl.ds(2 * hp, 2)
        zsend[part] = (acc1[part] + yrx[0, part].astype(F32)).astype(BF16)
        zx.append(go(rcopy(zsend.at[part], zrx.at[part], z_s.at[hp], z_r.at[hp], z_dev)))
    for hp in range(2):
        yx[1, hp].wait_recv()
    acc0[...] = acc0[...] + yrx[1].astype(F32)

    def nwait(rr, carry):
        for i, t in enumerate(row8):
            tc = lax.rem(t, 2)
            cp = rcopy(n_in.at[0, :, pl.ds(pl.multiple_of(rr * 512 + tc * 256, 256), 256)], nbuf.at[rr, x, c],
                       n_s.at[i, rr], n_r.at[i, rr], dev(x_=t // 2, c_=tc))
            cp.wait_send()
            cp.wait_recv()
        pltpu.make_async_copy(n_in.at[0, :, pl.ds(pl.multiple_of(rr * 512 + c * 256, 256), 256)],
                              nbuf.at[rr, x, c], nl_sem.at[rr]).wait()
        return carry

    lax.fori_loop(0, 8, nwait, 0)
    k2 = []
    for hp in range(2):
        zx[hp].wait_recv()
        part = pl.ds(2 * hp, 2)
        kga[part, pl.ds(c, 1)] = (acc0[part] + zrx[part].astype(F32)).astype(BF16).reshape(2, 1, 128, 256)
        mine = kga.at[part, c]
        k2.append(go(rcopy(mine, mine, kc2_s.at[hp], kc2_r.at[hp], core_dev)))
    ko = []
    for i, px in enumerate(xs):
        ko.append(go(rcopy(kga.at[px, c, :, pl.ds(0, 128)], kg_out.at[0, :, blk(x, 128)],
                           ko_s.at[0, i], ko_r.at[0, i], dev(x_=px))))
        ko.append(go(rcopy(kga.at[px, c, :, pl.ds(128, 128)], vg_out.at[0, :, blk(x, 128)],
                           ko_s.at[1, i], ko_r.at[1, i], dev(x_=px))))
    ko_own = [pltpu.make_async_copy(kga.at[x, c, :, pl.ds(0, 128)], kg_out.at[0, :, blk(x, 128)], l_sem.at[4]),
              pltpu.make_async_copy(kga.at[x, c, :, pl.ds(128, 128)], vg_out.at[0, :, blk(x, 128)], l_sem.at[5])]
    for cp in ko_own:
        cp.start()
    for cp in k2:
        cp.wait_recv()

    kgall = kga[...].reshape(1024, 256)
    w1 = []
    for d in range(4):
        py = lax.rem(y + d + 1, 4)
        for b in range(2):
            part = dot_tn(nbuf[py * 2 + b].reshape(1024, 256), kgall)
            w1s[d, b] = part.astype(BF16)
        if d < 3:
            w1.append(go(rcopy(w1s.at[d], w1r.at[d], w1_s.at[d], w1_r.at[d], ydev[d])))
    for cp in w1:
        cp.wait_recv()
    for b in range(2):
        t = w1s[3, b].astype(F32)
        for d in range(3):
            t = t + w1r[d, b].astype(F32)
        w2s[b] = t.astype(BF16).reshape(4, 4, 16, 256)
    w2 = []
    for i, pz in enumerate(zs):
        w2.append(go(rcopy(w2s.at[pz // 4, :, lax.rem(pz, 4)], w2r.at[i], w2_s.at[i], w2_r.at[i], zdev[i])))
    for cp in w2:
        cp.wait_recv()
    t = w2s[zh, :, pl.ds(zl, 1)].reshape(4, 16, 256).astype(F32)
    for i in range(7):
        t = t + w2r[i].astype(F32)
    w3s[...] = t
    self_core = x // 2

    def w4_copy(xl, cc_):
        return rcopy(w3s.at[xl * 2 + cc_], w4r.at[x], w4_s.at[xl * 2 + cc_], w4_r.at[x],
                     dev(x_=2 * c + xl, c_=cc_))

    for xl in range(2):
        for cc_ in range(2):
            is_me = (2 * c + xl == x) & (c == cc_)

            @pl.when(is_me)
            def _():
                w4r[pl.ds(x, 1)] = w3s[xl * 2 + cc_].reshape(1, 16, 256)

            @pl.when(jnp.logical_not(is_me))
            def _():
                w4_copy(xl, cc_).start()
    for xx in range(4):
        @pl.when(jnp.logical_not((x == xx) & (c == self_core)))
        def _():
            rcopy(w3s.at[0], w4r.at[xx], w4_s.at[0], w4_r.at[xx], core_dev).wait_recv()
    for xx in range(4):
        w_out[:, xx * 128:(xx + 1) * 128] = w4r[xx, :, 0:128]
        w_out[:, 512 + xx * 128:512 + (xx + 1) * 128] = w4r[xx, :, 128:256]
    for xl in range(2):
        for cc_ in range(2):
            @pl.when(jnp.logical_not((2 * c + xl == x) & (c == cc_)))
            def _():
                w4_copy(xl, cc_).wait_send()
    for h in range(4):
        for i in range(3):
            dq_copy(h, i).wait()
        dq_local(h).wait()
    for cp in ko:
        cp.wait_recv()
    for cp in ko_own:
        cp.wait()
    for cp in sends:
        cp.wait_send()


def local(query, keys, values, out_grad, normed_input, q_start, q_len):
    dma = pltpu.SemaphoreType.DMA
    V = pltpu.VMEM
    hbm = pl.BlockSpec(memory_space=pl.ANY)
    smem = pl.BlockSpec(memory_space=pltpu.SMEM)
    return pl.pallas_call(
        body,
        name="attention_grads",
        out_shape=(jax.ShapeDtypeStruct((1, 128, 2048), BF16), jax.ShapeDtypeStruct((1, 128, 512), BF16),
                   jax.ShapeDtypeStruct((1, 128, 512), BF16), jax.ShapeDtypeStruct((16, 1024), F32)),
        in_specs=[hbm] * 5 + [smem] * 2,
        out_specs=[hbm] * 3 + [pl.BlockSpec(memory_space=pltpu.VMEM)],
        scratch_shapes=[
            V((4, 128, 512), BF16), V((4, 128, 512), BF16), V((2, 2, 4, 256, 256), BF16),
            V((8, 4, 2, 128, 256), BF16),
            V((3584, 256), F32), V((3584, 256), F32), V((4096, 128), F32), V((4096, 128), F32),
            V((4, 128, 512), BF16),
            V((4, 4, 128, 256), BF16), V((4, 4, 128, 256), BF16),
            V((2, 4, 128, 256), BF16), V((2, 4, 128, 256), BF16),
            V((4, 128, 256), F32), V((4, 128, 256), F32), V((4, 128, 256), BF16), V((4, 128, 256), BF16),
            V((4, 2, 128, 256), BF16),
            V((4, 2, 256, 256), BF16), V((3, 2, 256, 256), BF16), V((2, 4, 4, 16, 256), BF16),
            V((7, 4, 16, 256), BF16), V((4, 16, 256), F32), V((4, 16, 256), F32),
            dma((2, 3)), dma((2, 3)), dma((2, 3)), dma((2, 3)), dma((4,)), dma((4,)), dma((2, 4)), dma((2, 4)),
            dma((4, 4)), dma((4, 4)), dma((7, 8)), dma((7, 8)), dma((4, 3)), dma((4, 3)),
            dma((4,)), dma((4,)), dma((2, 2)), dma((2, 2)), dma((2,)), dma((2,)), dma((2,)), dma((2,)),
            dma((2, 3)), dma((2, 3)),
            dma((3,)), dma((3,)), dma((7,)), dma((7,)), dma((4,)), dma((4,)), dma((6,)), dma((8,)), dma((4,)),
        ],
        compiler_params=pltpu.CompilerParams(collective_id=0, has_side_effects=True, vmem_limit_bytes=56 << 20),
    )(query, out_grad, keys, values, normed_input, q_start, q_len)


def solution(mesh):
    tok = P("dp", "seq", None)
    return jax.shard_map(
        local, mesh=mesh,
        in_specs=(tok, tok, tok, tok, tok, P("dp"), P("dp")),
        out_specs=(tok, tok, tok, P(("seq", "dp"), None)),
        check_vma=False)
```

time: 1880 us -> 115 us (0.06)
  waiting for transfers between devices: 1470 us -> 0 us
  local copies, waits for them, and re-layouts: 120 us -> 4.36 us
  Pallas kernels: 0 us -> 110 us
  matrix products: 109 us -> 0 us
  other arithmetic: 66.8 us -> 0 us
  starting transfers between devices: 65.9 us -> 0 us
    unnamed x2 -> x0, waiting for transfers between devices: 1270 us -> none
    all_to_all x6 -> x0, waiting for transfers between devices: 209 us -> none  [the longest x1 51 us: local(): lax.all_to_all(key_units, 'seq', split_axis=1, concat_axis=0, tiled=True)]
    pallas_call x0 -> x1, Pallas kernels: none -> 110 us  [local(): pl.pallas_call(body, name='attention_grads', out_shape=(jax.ShapeDtypeStr...]
    dot_general x21 -> x0, matrix products: 109 us -> none  [the longest x4 37.7 us: one_block(): jnp.einsum('qhd,khd->hqk', grad_block, value_block, preferred_element_typ...]
    all_to_all x6 -> x0, starting transfers between devices: 65.9 us -> none  [the longest x1 25.4 us: local(): lax.all_to_all(value_acc.reshape(seq_count, tokens_dev, 1, width_dev).ast...]
    convert_element_type x6 -> x0, other arithmetic: 44.8 us -> none  [the longest x4 40.1 us: one_block(): (probability * (dprob - row_delta) * score_scale).astype(jnp.bfloat16)]
    dynamic_slice x24 -> x0, local copies, waits for them, and re-layouts: 39.3 us -> none  [the longest x8 19.9 us: one_block(): lax.dynamic_slice_in_dim(value_acc, key_first, seq_len, 0)]
    dynamic_update_slice x20 -> x0, local copies, waits for them, and re-layouts: 39.1 us -> none  [the longest x8 28.5 us: one_block(): lax.dynamic_update_slice_in_dim(value_acc, value_part, key_first, 0)]
  transfers between devices with their start and end apart: 7 -> 0, of which waited for: 7 -> 0; matrix products, arithmetic and copies ran while one was open for 1% -> 0% of each run, Pallas kernels for 0% -> 0%
where the time goes in v2:
time: 115 us
  Pallas kernels  110 us (96%)
  local copies, waits for them, and re-layouts  4.36 us (4%)
    pallas_call x1, Pallas kernels, local(): pl.pallas_call(body, name='attention_grads', out_shape=(jax.ShapeDtypeStr...  110 us
    unnamed x10, local copies, waits for them, and re-layouts  4.36 us

profile of v2, /device:TPU:1, one launch (start us, length us, event | category | flops | bytes accessed | tf_op | source)
XLA Modules:
  0.0 114.5 jit_solution(7133768161957097511)
XLA Ops:
  0.6 109.5 %attention_grads.1 = (bf16[1,128,2048]{2,1,0:T(8,128)(2,1)}, bf16[1,128,512]{2,1,0:T(8,128)(2,1)}, bf16[1,128,512]{2,1,0:T(8,128)(2,1)}, f32[16,1024]{1,0:T(8,128)}) custom-call(bf16[1,128,2048]{2,1,0:T(8,128)(2,1)} %q_in.1, bf16[1,128,2048]{2,1,0:T(8,128)(2,1)} %g_in.1, bf16[1,128,512]{2,1,0:T(8,128)(2,1)} %k_in.1, bf16[1,128,512]{2,1,0:T(8,128)(2,1)} %v_in.1, ...), custom_call_target="tpu_custom_call" | custom-call | tf_op jit(solution)/shard_map/attention_grads/pallas_call | solution.py:388
  110.1 0.0 copy-start.1
  110.2 1.9 %copy.15 = bf16[1,128,2048]{2,1,0:T(8,128)(2,1)} copy(bf16[1,128,2048]{2,1,0:T(8,128)(2,1)} %get-tuple-element.8) | data formatting | bytes 1048576
  112.1 0.0 copy-done.1
  112.1 0.0 copy-start
  112.1 0.7 copy.16
  112.7 0.3 copy-done
  113.0 0.0 copy-start.2
  113.0 0.7 copy.17
  113.7 0.2 copy-done.2
  113.9 0.6 copy.18
Async XLA Ops:
  110.1 1.9 %copy-start.1 = (bf16[1,128,512]{2,1,0:T(8,128)(2,1)S(1)}, bf16[1,128,512]{2,1,0:T(8,128)(2,1)}, u32[]{:S(2)}) copy-start(bf16[1,128,512]{2,1,0:T(8,128)(2,1)} %get-tuple-element.9) | copy-start | bytes 393220
  112.1 1.0 copy-start
  113.0 0.9 copy-start.2

commit v3 on v2

v3 whole, which is shorter than its diff:
```python
import math
import jax
import jax.numpy as jnp
from jax import lax
from jax.experimental import pallas as pl
from jax.experimental.pallas import tpu as pltpu
from jax.sharding import PartitionSpec as P

HEAD_DIM = 128
SCALE = 1.0 / math.sqrt(HEAD_DIM)
EXPC = SCALE * math.log2(math.e)
NEG = -1e30
F32 = jnp.float32
BF16 = jnp.bfloat16
CK = 512


def dot_nt(a, b):
    return lax.dot_general(a, b, (((1,), (1,)), ((), ())), preferred_element_type=F32)


def dot_nn(a, b):
    return lax.dot_general(a, b, (((1,), (0,)), ((), ())), preferred_element_type=F32)


def dot_tn(a, b):
    return lax.dot_general(a, b, (((0,), (0,)), ((), ())), preferred_element_type=F32)


def coords():
    seq = lax.axis_index("seq")
    c = lax.rem(seq, 2)
    x = lax.rem(seq // 2, 4)
    zh = lax.rem(seq // 8, 2)
    yl = lax.rem(seq // 16, 2)
    s = seq // 32
    zl = lax.axis_index("dp")
    return s, yl, zh, x, c, zl


def seq_of(s, yl, zh, x, c):
    return s * 32 + yl * 16 + zh * 8 + x * 2 + c


def rcopy(src, dst, ssem, rsem, dev):
    return pltpu.make_async_remote_copy(
        src_ref=src, dst_ref=dst, send_sem=ssem, recv_sem=rsem,
        device_id={"seq": dev[0], "dp": dev[1]}, device_id_type=pl.DeviceIdType.MESH)


def greet(peers):
    barrier = pltpu.get_barrier_semaphore()
    for seq, dp in peers:
        pl.semaphore_signal(barrier, inc=1, device_id={"seq": seq, "dp": dp},
                            device_id_type=pl.DeviceIdType.MESH)
    pl.semaphore_wait(barrier, len(peers))


def blk(i, w):
    return pl.ds(pl.multiple_of(i * w, w), w)


def body(q_in, g_in, k_in, v_in, n_in, start_ref, len_ref,
         dq_out, kg_out, vg_out, w_out,
         q_ref, g_ref, kv, nbuf, s_ref, d_ref, dk_ref, dv_ref, dq_ref,
         csend, crx, ysend, yrx, acc0, acc1, zsend, zrx, kga,
         w1s, w1r, w1o, kt_ref, st, fac, dlt, dqa, w2s, w2r, w3s, w4r,
         kx_s, kx_r, qx_s, qx_r, kz_s, kz_r, ky_s, ky_r, kc_s, kc_r, n_s, n_r, nf_s, nf_r, nc_s, nc_r, dq_s, dq_r,
         c_s, c_r, y_s, y_r, z_s, z_r, kc2_s, kc2_r, ko_s, ko_r,
         w1_s, w1_r, w2_s, w2_r, w4_s, w4_r, l_sem, nl_sem, dql_sem):
    s, yl, zh, x, c, zl = coords()
    y = s * 2 + yl
    z = zh * 4 + zl
    me8 = x * 2 + c

    def dev(s_=None, yl_=None, zh_=None, x_=None, c_=None, zl_=None):
        return (seq_of(s if s_ is None else s_, yl if yl_ is None else yl_, zh if zh_ is None else zh_,
                       x if x_ is None else x_, c if c_ is None else c_), zl if zl_ is None else zl_)

    row8 = [lax.rem(me8 + d, 8) for d in range(1, 8)]
    xs = [lax.rem(x + d, 4) for d in range(1, 4)]
    ys = [lax.rem(y + d, 4) for d in range(1, 4)]
    zs = [lax.rem(z + d, 8) for d in range(1, 8)]
    ydev = [dev(s_=p // 2, yl_=lax.rem(p, 2)) for p in ys]
    zdev = [dev(zh_=p // 4, zl_=lax.rem(p, 4)) for p in zs]
    core_dev = dev(c_=1 - c)
    y_dev = dev(yl_=1 - yl)
    z_dev = dev(zh_=1 - zh)
    greet([dev(x_=p // 2, c_=lax.rem(p, 2)) for p in row8] + ydev + zdev)

    sends = []

    def go(cp):
        cp.start()
        sends.append(cp)
        return cp

    crow = blk(c, 128)
    last = yl * zh

    def slot(yl_, zh_, plane):
        return jnp.where(yl_ == 0, jnp.where(zh_ == plane, 0, 1), 2 + zh_)

    mine = slot(yl, zh, zh)
    kx = []
    for i, px in enumerate(xs):
        kx.append((go(rcopy(k_in.at[0, :, blk(px, 128)], kv.at[mine, x, crow, pl.ds(0, 128)],
                            kx_s.at[0, i], kx_r.at[0, i], dev(x_=px))),
                   go(rcopy(v_in.at[0, :, blk(px, 128)], kv.at[mine, x, crow, pl.ds(128, 128)],
                            kx_s.at[1, i], kx_r.at[1, i], dev(x_=px)))))
    own_kv = [pltpu.make_async_copy(k_in.at[0, :, blk(x, 128)], kv.at[mine, x, crow, pl.ds(0, 128)], l_sem.at[0]),
              pltpu.make_async_copy(v_in.at[0, :, blk(x, 128)], kv.at[mine, x, crow, pl.ds(128, 128)], l_sem.at[1])]
    own_q = [pltpu.make_async_copy(q_in.at[0, :, blk(x, 512)], q_ref.at[x], l_sem.at[2]),
             pltpu.make_async_copy(g_in.at[0, :, blk(x, 512)], g_ref.at[x], l_sem.at[3])]
    for cp in own_kv + own_q:
        cp.start()

    def q_send(ph):
        out = []
        for i, px in enumerate(xs):
            src = pl.ds(pl.multiple_of(px * 512 + ph * 256, 256), 256)
            dst = pl.ds(ph * 256, 256)
            out.append(go(rcopy(q_in.at[0, :, src], q_ref.at[x, :, dst], qx_s.at[ph, 0, i], qx_r.at[ph, 0, i], dev(x_=px))))
            out.append(go(rcopy(g_in.at[0, :, src], g_ref.at[x, :, dst], qx_s.at[ph, 1, i], qx_r.at[ph, 1, i], dev(x_=px))))
        return out

    qx0 = q_send(0)

    def piece(sl, k):
        return kv.at[sl, lax.rem(x - k + 4, 4), crow]

    zc, y0, y1 = [], [], []
    cc = [[], [], [], []]

    def to_core(e, k, p):
        cc[e].append(go(rcopy(p, p, kc_s.at[e, k], kc_r.at[e, k], core_dev)))

    for k in range(4):
        for cp in (own_kv if k == 0 else kx[k - 1]):
            cp.wait() if k == 0 else cp.wait_recv()
        zc.append(go(rcopy(piece(mine, k), piece(slot(yl, zh, 1 - zh), k), kz_s.at[k], kz_r.at[k], z_dev)))
        y0.append(go(rcopy(piece(mine, k), piece(mine, k), ky_s.at[0, k], ky_r.at[0, k], y_dev)))
        to_core(0, k, piece(mine, k))
    ev = [mine, slot(1 - yl, zh, zh), slot(yl, 1 - zh, zh), slot(1 - yl, 1 - zh, zh)]

    dk_ref[...] = jnp.zeros_like(dk_ref)
    dv_ref[...] = jnp.zeros_like(dv_ref)
    st[:, 0] = jnp.full((8, 16, 256), NEG, F32)
    st[:, 1:3] = jnp.zeros((8, 2, 16, 256), F32)
    dqa[...] = jnp.zeros_like(dqa)
    start = start_ref[s]
    end = start + len_ref[s]
    lane = lax.broadcasted_iota(jnp.int32, (1, 256), 1)

    def keys(j, n):
        if isinstance(j, int):
            return kv[j // 4, j % 4:j % 4 + n].reshape(n * 256, 256)[:, 0:128]
        return kv[j // 4, pl.ds(lax.rem(j, 4), n), :, 0:128].reshape(n * 256, 128)

    def values(j):
        return kv[j // 4, j % 4, :, 128:256]

    def rows_of(j, n=1):
        return pl.ds(j * 256 if isinstance(j, int) else pl.multiple_of(j * 256, 256), n * 256)

    def unit(u):
        h, half = u // 2, (u % 2 if isinstance(u, int) else lax.rem(u, 2))
        cols = pl.ds(h * 128 if isinstance(h, int) else pl.multiple_of(h * 128, 128), 128)
        xx = pl.ds(2 * half, 2)
        pos = yl * 2048 + zh * 1024 + (2 * half + lane // 128) * 256 + c * 128 + lax.rem(lane, 128)
        lim = jnp.maximum(start, jnp.minimum(end, pos + 1))
        return q_ref[xx, :, cols].reshape(256, 128), g_ref[xx, :, cols].reshape(256, 128), lim

    def dq_store(u, dq):
        h, half = u // 2, (u % 2 if isinstance(u, int) else lax.rem(u, 2))
        cols = pl.ds(h * 128 if isinstance(h, int) else pl.multiple_of(h * 128, 128), 128)
        dq_ref[pl.ds(2 * half, 2), :, cols] = (dq.T * SCALE).astype(BF16).reshape(2, 128, 128)

    def pass12(u, su, j, masked):
        q, g, lim = unit(u)
        rows = rows_of(j)
        sc = dot_nt(kv[j // 4, (j % 4 if isinstance(j, int) else lax.rem(j, 4)), :, 0:128], q)
        if masked:
            kpos = lax.broadcasted_iota(jnp.int32, (256, 256), 0)
            sc = jnp.where(kpos < lim - j * 256, sc, NEG)
        m = jnp.max(sc, axis=0, keepdims=True)
        e = jnp.exp2((sc - m) * EXPC)
        dp = dot_nt(kv[j // 4, (j % 4 if isinstance(j, int) else lax.rem(j, 4)), :, 128:256], g)
        st[u, 0, pl.ds(j, 1)] = m
        st[u, 1, pl.ds(j, 1)] = jnp.sum(e, axis=0, keepdims=True)
        st[u, 2, pl.ds(j, 1)] = jnp.sum(e * dp, axis=0, keepdims=True)
        s_ref[su, rows, :] = e
        d_ref[su, rows, :] = dp

    def finish(u, su):
        m = jnp.max(st[u, 0], axis=0, keepdims=True)
        f = jnp.exp2((st[u, 0] - m) * EXPC)
        f = f * (1.0 / jnp.sum(st[u, 1] * f, axis=0, keepdims=True))
        fac[su] = f
        dlt[su] = jnp.sum(st[u, 2] * f, axis=0, keepdims=True)

    def pass3(u, su, j, n, dq):
        q, g, _ = unit(u)
        dlv = dlt[su]
        ds_, p_ = [], []
        for i in range(n):
            r = rows_of(j + i)
            p = s_ref[su, r, :] * fac[su, pl.ds(j + i, 1)]
            ds_.append((p * (d_ref[su, r, :] - dlv)).astype(BF16))
            p_.append(p.astype(BF16))
        ds = ds_[0] if n == 1 else jnp.concatenate(ds_, axis=0)
        p = p_[0] if n == 1 else jnp.concatenate(p_, axis=0)
        rows = rows_of(j, n)
        dk_ref[rows, :] += dot_nn(ds, q)
        dv_ref[rows, :] += dot_nn(p, g)
        return dq + dot_nn(kt_ref[:, rows], ds)

    def arrive(e):
        sl = ev[e]

        def one(b, carry):
            j = sl * 4 + b
            kt_ref[:, rows_of(j)] = keys(j, 1).T
            for u in range(4):
                pass12(u, u, j, True)
            return carry
        lax.fori_loop(0, jnp.where(sl < 3, 4, 2 * last), one, 0)

    for k in range(4):
        y0[k].wait_recv()
        to_core(1, k, piece(ev[1], k))
    for cp in own_q:
        cp.wait()
    for cp in qx0:
        cp.wait_recv()
    qx1 = q_send(1)
    for cp in cc[0]:
        cp.wait_recv()
    arrive(0)

    def n_copy(rr, side, cc_):
        px = lax.rem(x + (1 if side == 0 else 3), 4)
        return rcopy(n_in.at[0, :, pl.ds(pl.multiple_of(rr * 512 + cc_ * 256, 256), 256)], nbuf.at[rr, x, c],
                     n_s.at[side, cc_, rr], n_r.at[side, c, rr], dev(x_=px, c_=cc_))

    def n_fwd(i, side, cc_):
        rr = i + 4 * side
        src = nbuf.at[rr, lax.rem(x + (3 if side == 0 else 1), 4), cc_]
        px = lax.rem(x + (1 if side == 0 else 3), 4)
        return rcopy(src, src, nf_s.at[side, cc_, i], nf_r.at[side, cc_, i], dev(x_=px))

    def n_core(rr):
        return rcopy(n_in.at[0, :, pl.ds(pl.multiple_of(rr * 512 + (1 - c) * 256, 256), 256)], nbuf.at[rr, x, c],
                     nc_s.at[rr], nc_r.at[rr], core_dev)

    def n_local(rr):
        return pltpu.make_async_copy(n_in.at[0, :, pl.ds(pl.multiple_of(rr * 512 + c * 256, 256), 256)],
                                     nbuf.at[rr, x, c], nl_sem.at[rr])

    def nsend(i, carry):
        for cc_ in range(2):
            n_copy(i, 0, cc_).start()
            n_copy(lax.rem(i + 4, 8), 1, cc_).start()
        n_core(i).start()
        n_local(i).start()
        return carry

    for k in range(2):
        zc[k].wait_recv()
        p = piece(ev[2], k)
        y1.append(go(rcopy(p, piece(slot(yl, 1 - zh, zh), k), ky_s.at[1, k], ky_r.at[1, k], y_dev)))
        to_core(2, k, p)
    lax.fori_loop(0, 8, nsend, 0)
    for cp in cc[1]:
        cp.wait_recv()
    arrive(1)
    for k in range(2, 4):
        zc[k].wait_recv()
        p = piece(ev[2], k)
        y1.append(go(rcopy(p, piece(slot(yl, 1 - zh, zh), k), ky_s.at[1, k], ky_r.at[1, k], y_dev)))
        to_core(2, k, p)
    for k in range(4):
        y1[k].wait_recv()
        to_core(3, k, piece(ev[3], k))
    for cp in cc[2]:
        cp.wait_recv()
    arrive(2)
    for cp in cc[3]:
        cp.wait_recv()
    arrive(3)
    for u in range(4):
        finish(u, u)
    for cp in qx1:
        cp.wait_recv()

    def mid(u, carry):
        dq = jnp.zeros((128, 256), F32)
        for j in range(12):
            dq = pass3(u, u, j, 1, dq)
            pass12(u + 4, u, j, j >= 8)
        dqa[4] = dq

        @pl.when(last == 1)
        def _():
            d2 = dqa[4]
            for j in range(12, 14):
                d2 = pass3(u, u, j, 1, d2)
                pass12(u + 4, u, j, True)
            dqa[4] = d2
        dq_store(u, dqa[4])
        finish(u + 4, u)
        return carry

    lax.fori_loop(0, 3, mid, 0)

    def fwd(i, carry):
        for side in range(2):
            for cc_ in range(2):
                rcopy(nbuf.at[0, 0, 0], nbuf.at[i + 4 * side, x, cc_], n_s.at[side, cc_, i],
                      n_r.at[side, cc_, i + 4 * side], core_dev).wait_recv()
                n_fwd(i, side, cc_).start()
        return carry

    lax.fori_loop(0, 4, fwd, 0)
    lax.fori_loop(3, 4, mid, 0)

    def dq_copy(h, i):
        px = xs[i]
        return rcopy(dq_ref.at[px, :, blk(h, 128)], dq_out.at[0, :, blk(x * 4 + h, 128)],
                     dq_s.at[h, i], dq_r.at[h, i], dev(x_=px))

    def dq_local(h):
        return pltpu.make_async_copy(dq_ref.at[x, :, blk(h, 128)], dq_out.at[0, :, blk(x * 4 + h, 128)],
                                     dql_sem.at[h])

    def dq_send(h):
        for i in range(3):
            dq_copy(h, i).start()
        dq_local(h).start()

    dq_send(0)
    dq_send(1)

    def back(sl, trips):
        def two(b, carry):
            for u in range(4):
                dqa[u] = pass3(u + 4, u, sl * 4 + 2 * b, 2, dqa[u])
            return carry
        lax.fori_loop(0, trips, two, 0)

    def grads(yl_, zh_, x_, c_):
        r = pl.ds(pl.multiple_of((slot(yl_, zh_, zh) * 4 + x_) * 256 + c_ * 128, 128), 128)
        return jnp.concatenate([dk_ref[r, :] * SCALE, dv_ref[r, :]], axis=1)

    quad = [(1 - yl, 1 - zh), (yl, 1 - zh), (1 - yl, zh), (yl, zh)]
    cx = []

    def core_send(k):
        for x_ in range(4):
            csend[k, x_] = grads(quad[k][0], quad[k][1], x_, 1 - c).astype(BF16)
        cx.append(go(rcopy(csend.at[k], crx.at[k], c_s.at[k], c_r.at[k], core_dev)))

    def pair(k, x_):
        return grads(quad[k][0], quad[k][1], x_, c) + crx[k, x_].astype(F32)

    yx = {}

    def y_stage(k, sl):
        cx[k].wait_recv()
        for hp in range(2):
            for x_ in (2 * hp, 2 * hp + 1):
                ysend[sl, x_] = pair(k, x_).astype(BF16)
            part = pl.ds(2 * hp, 2)
            yx[sl, hp] = go(rcopy(ysend.at[sl, part], yrx.at[sl, part], y_s.at[sl, hp], y_r.at[sl, hp], y_dev))

    back(1, 2)
    back(2, 2 * zh)
    core_send(0)
    core_send(1)
    back(0, 2)
    y_stage(0, 0)
    cx[1].wait_recv()
    for x_ in range(4):
        acc1[x_] = pair(1, x_)
    back(2, 2 * (1 - zh))
    back(3, last)
    core_send(2)
    core_send(3)
    zx = []
    for hp in range(2):
        yx[0, hp].wait_recv()
        part = pl.ds(2 * hp, 2)
        zsend[part] = (acc1[part] + yrx[0, part].astype(F32)).astype(BF16)
        zx.append(go(rcopy(zsend.at[part], zrx.at[part], z_s.at[hp], z_r.at[hp], z_dev)))
    y_stage(2, 1)
    for u in range(4):
        dq_store(u + 4, dqa[u])
    dq_send(2)
    dq_send(3)
    cx[3].wait_recv()
    for x_ in range(4):
        acc0[x_] = pair(3, x_)
    for hp in range(2):
        yx[1, hp].wait_recv()
    acc0[...] = acc0[...] + yrx[1].astype(F32)

    def nwait(i, carry):
        for cc_ in range(2):
            for side in range(2):
                n_copy(i, side, cc_).wait_send()
        n_core(i).wait()
        n_local(i).wait()
        return carry

    def nwait4(i, carry):
        for side in range(2):
            for cc_ in range(2):
                rr = i + 4 * (1 - side)
                rcopy(nbuf.at[0, 0, 0], nbuf.at[rr, x, cc_], n_s.at[side, cc_, i],
                      n_r.at[side, cc_, rr], core_dev).wait_recv()
                n_fwd(i, side, cc_).wait()
        return carry

    lax.fori_loop(0, 8, nwait, 0)
    lax.fori_loop(0, 4, nwait4, 0)
    k2 = []
    for hp in range(2):
        zx[hp].wait_recv()
        part = pl.ds(2 * hp, 2)
        kga[part, pl.ds(c, 1)] = (acc0[part] + zrx[part].astype(F32)).astype(BF16).reshape(2, 1, 128, 256)
        own = kga.at[part, c]
        k2.append(go(rcopy(own, own, kc2_s.at[hp], kc2_r.at[hp], core_dev)))
    ko = []
    for i, px in enumerate(xs):
        ko.append(go(rcopy(kga.at[px, c, :, pl.ds(0, 128)], kg_out.at[0, :, blk(x, 128)],
                           ko_s.at[0, i], ko_r.at[0, i], dev(x_=px))))
        ko.append(go(rcopy(kga.at[px, c, :, pl.ds(128, 128)], vg_out.at[0, :, blk(x, 128)],
                           ko_s.at[1, i], ko_r.at[1, i], dev(x_=px))))
    ko_own = [pltpu.make_async_copy(kga.at[x, c, :, pl.ds(0, 128)], kg_out.at[0, :, blk(x, 128)], l_sem.at[4]),
              pltpu.make_async_copy(kga.at[x, c, :, pl.ds(128, 128)], vg_out.at[0, :, blk(x, 128)], l_sem.at[5])]
    for cp in ko_own:
        cp.start()
    for cp in k2:
        cp.wait_recv()

    kgall = kga[...].reshape(1024, 256)
    border = [1 - zh, zh]
    w1 = {}
    for bi, b in enumerate(border):
        for d in range(3):
            py = lax.rem(y + d + 1, 4)
            w1s[d, bi] = dot_tn(nbuf[py * 2 + b].reshape(1024, 256), kgall).astype(BF16)
            w1[d, bi] = go(rcopy(w1s.at[d, bi], w1r.at[d, bi], w1_s.at[d, bi], w1_r.at[d, bi], ydev[d]))
    for bi, b in enumerate(border):
        w1o[bi] = dot_tn(nbuf[y * 2 + b].reshape(1024, 256), kgall)
    w2 = []
    for bi, b in enumerate(border):
        for d in range(3):
            w1[d, bi].wait_recv()
        t = w1o[bi]
        for d in range(3):
            t = t + w1r[d, bi].astype(F32)
        w2s[bi] = t.astype(BF16).reshape(4, 4, 16, 256)
        for i in range(bi, 4):
            pz = lax.rem(zl + i, 4)
            sl = i if bi == 0 else 3 + i
            w2.append(go(rcopy(w2s.at[bi, :, pz], w2r.at[sl], w2_s.at[sl], w2_r.at[sl],
                               dev(zh_=b, zl_=pz))))
    for cp in w2:
        cp.wait_recv()
    t = w2s[1, :, pl.ds(zl, 1)].reshape(4, 16, 256).astype(F32)
    for i in range(7):
        t = t + w2r[i].astype(F32)
    w3s[...] = t
    self_core = x // 2

    def w4_copy(xl, cc_):
        return rcopy(w3s.at[xl * 2 + cc_], w4r.at[x], w4_s.at[xl * 2 + cc_], w4_r.at[x],
                     dev(x_=2 * c + xl, c_=cc_))

    for xl in range(2):
        for cc_ in range(2):
            is_me = (2 * c + xl == x) & (c == cc_)

            @pl.when(is_me)
            def _():
                w4r[pl.ds(x, 1)] = w3s[xl * 2 + cc_].reshape(1, 16, 256)

            @pl.when(jnp.logical_not(is_me))
            def _():
                w4_copy(xl, cc_).start()
    for xx in range(4):
        @pl.when(jnp.logical_not((x == xx) & (c == self_core)))
        def _():
            rcopy(w3s.at[0], w4r.at[xx], w4_s.at[0], w4_r.at[xx], core_dev).wait_recv()
    for xx in range(4):
        w_out[:, xx * 128:(xx + 1) * 128] = w4r[xx, :, 0:128]
        w_out[:, 512 + xx * 128:512 + (xx + 1) * 128] = w4r[xx, :, 128:256]
    for xl in range(2):
        for cc_ in range(2):
            @pl.when(jnp.logical_not((2 * c + xl == x) & (c == cc_)))
            def _():
                w4_copy(xl, cc_).wait_send()
    for h in range(4):
        for i in range(3):
            dq_copy(h, i).wait()
        dq_local(h).wait()
    for cp in ko:
        cp.wait_recv()
    for cp in ko_own:
        cp.wait()
    for cp in sends:
        cp.wait_send()


def local(query, keys, values, out_grad, normed_input, q_start, q_len):
    dma = pltpu.SemaphoreType.DMA
    V = pltpu.VMEM
    hbm = pl.BlockSpec(memory_space=pl.ANY)
    smem = pl.BlockSpec(memory_space=pltpu.SMEM)
    return pl.pallas_call(
        body,
        name="attention_grads",
        out_shape=(jax.ShapeDtypeStruct((1, 128, 2048), BF16), jax.ShapeDtypeStruct((1, 128, 512), BF16),
                   jax.ShapeDtypeStruct((1, 128, 512), BF16), jax.ShapeDtypeStruct((16, 1024), F32)),
        in_specs=[hbm] * 5 + [smem] * 2,
        out_specs=[hbm] * 3 + [pl.BlockSpec(memory_space=pltpu.VMEM)],
        scratch_shapes=[
            V((4, 128, 512), BF16), V((4, 128, 512), BF16), V((4, 4, 256, 256), BF16),
            V((8, 4, 2, 128, 256), BF16),
            V((4, 3584, 256), F32), V((4, 3584, 256), F32), V((4096, 128), F32), V((4096, 128), F32),
            V((4, 128, 512), BF16),
            V((4, 4, 128, 256), BF16), V((4, 4, 128, 256), BF16),
            V((2, 4, 128, 256), BF16), V((2, 4, 128, 256), BF16),
            V((4, 128, 256), F32), V((4, 128, 256), F32), V((4, 128, 256), BF16), V((4, 128, 256), BF16),
            V((4, 2, 128, 256), BF16),
            V((3, 2, 256, 256), BF16), V((3, 2, 256, 256), BF16), V((2, 256, 256), F32),
            V((128, 4096), BF16), V((8, 3, 16, 256), F32), V((4, 16, 256), F32), V((4, 1, 256), F32),
            V((5, 128, 256), F32), V((2, 4, 4, 16, 256), BF16),
            V((7, 4, 16, 256), BF16), V((4, 16, 256), F32), V((4, 16, 256), F32),
            dma((2, 3)), dma((2, 3)), dma((2, 2, 3)), dma((2, 2, 3)), dma((4,)), dma((4,)), dma((2, 4)), dma((2, 4)),
            dma((4, 4)), dma((4, 4)), dma((2, 2, 8)), dma((2, 2, 8)), dma((2, 2, 4)), dma((2, 2, 4)),
            dma((8,)), dma((8,)), dma((4, 3)), dma((4, 3)),
            dma((4,)), dma((4,)), dma((2, 2)), dma((2, 2)), dma((2,)), dma((2,)), dma((2,)), dma((2,)),
            dma((2, 3)), dma((2, 3)),
            dma((3, 2)), dma((3, 2)), dma((7,)), dma((7,)), dma((4,)), dma((4,)), dma((6,)), dma((8,)), dma((4,)),
        ],
        compiler_params=pltpu.CompilerParams(collective_id=0, has_side_effects=True, vmem_limit_bytes=60 << 20),
    )(query, out_grad, keys, values, normed_input, q_start, q_len)


def solution(mesh):
    tok = P("dp", "seq", None)
    return jax.shard_map(
        local, mesh=mesh,
        in_specs=(tok, tok, tok, tok, tok, P("dp"), P("dp")),
        out_specs=(tok, tok, tok, P(("seq", "dp"), None)),
        check_vma=False)
```

time: 115 us -> 105 us (0.913)
  Pallas kernels: 110 us -> 99.5 us
    pallas_call x1, Pallas kernels: 110 us -> 99.5 us  [local(): pl.pallas_call(body, name='attention_grads', out_shape=(jax.ShapeDtypeStr...]
where the time goes in v3:
time: 105 us
  Pallas kernels  99.5 us (95%)
  local copies, waits for them, and re-layouts  4.36 us (4%)
    pallas_call x1, Pallas kernels, local(): pl.pallas_call(body, name='attention_grads', out_shape=(jax.ShapeDtypeStr...  99.5 us
    unnamed x10, local copies, waits for them, and re-layouts  4.36 us

profile of v3, /device:TPU:1, one launch (start us, length us, event | category | flops | bytes accessed | tf_op | source)
XLA Modules:
  0.0 104.5 jit_solution(12464878194740446584)
XLA Ops:
  0.6 99.5 %attention_grads.1 = (bf16[1,128,2048]{2,1,0:T(8,128)(2,1)}, bf16[1,128,512]{2,1,0:T(8,128)(2,1)}, bf16[1,128,512]{2,1,0:T(8,128)(2,1)}, f32[16,1024]{1,0:T(8,128)}) custom-call(bf16[1,128,2048]{2,1,0:T(8,128)(2,1)} %q_in.1, bf16[1,128,2048]{2,1,0:T(8,128)(2,1)} %g_in.1, bf16[1,128,512]{2,1,0:T(8,128)(2,1)} %k_in.1, bf16[1,128,512]{2,1,0:T(8,128)(2,1)} %v_in.1, ...), custom_call_target="tpu_custom_call" | custom-call | tf_op jit(solution)/shard_map/attention_grads/pallas_call | solution.py:521
  100.1 0.0 copy-start.1
  100.2 1.9 %copy.15 = bf16[1,128,2048]{2,1,0:T(8,128)(2,1)} copy(bf16[1,128,2048]{2,1,0:T(8,128)(2,1)} %get-tuple-element.8) | data formatting | bytes 1048576
  102.1 0.0 copy-done.1
  102.1 0.0 copy-start
  102.1 0.7 copy.16
  102.7 0.3 copy-done
  103.0 0.0 copy-start.2
  103.0 0.7 copy.17
  103.7 0.2 copy-done.2
  103.9 0.6 copy.18
Async XLA Ops:
  100.1 1.9 %copy-start.1 = (bf16[1,128,512]{2,1,0:T(8,128)(2,1)S(1)}, bf16[1,128,512]{2,1,0:T(8,128)(2,1)}, u32[]{:S(2)}) copy-start(bf16[1,128,512]{2,1,0:T(8,128)(2,1)} %get-tuple-element.9) | copy-start | bytes 393220
  102.1 1.0 copy-start
  103.0 0.9 copy-start.2

commit v4 on v3

v4 whole, which is shorter than its diff:
```python
import math
import jax
import jax.numpy as jnp
from jax import lax
from jax.experimental import pallas as pl
from jax.experimental.pallas import tpu as pltpu
from jax.sharding import PartitionSpec as P

HEAD_DIM = 128
SCALE = 1.0 / math.sqrt(HEAD_DIM)
EXPC = SCALE * math.log2(math.e)
NEG = -1e30
F32 = jnp.float32
BF16 = jnp.bfloat16


def dot_nt(a, b):
    return lax.dot_general(a, b, (((1,), (1,)), ((), ())), preferred_element_type=F32)


def dot_nn(a, b):
    return lax.dot_general(a, b, (((1,), (0,)), ((), ())), preferred_element_type=F32)


def dot_tn(a, b):
    return lax.dot_general(a, b, (((0,), (0,)), ((), ())), preferred_element_type=F32)


def coords():
    seq = lax.axis_index("seq")
    c = lax.rem(seq, 2)
    x = lax.rem(seq // 2, 4)
    zh = lax.rem(seq // 8, 2)
    yl = lax.rem(seq // 16, 2)
    s = seq // 32
    zl = lax.axis_index("dp")
    return s, yl, zh, x, c, zl


def seq_of(s, yl, zh, x, c):
    return s * 32 + yl * 16 + zh * 8 + x * 2 + c


def rcopy(src, dst, ssem, rsem, dev):
    return pltpu.make_async_remote_copy(
        src_ref=src, dst_ref=dst, send_sem=ssem, recv_sem=rsem,
        device_id={"seq": dev[0], "dp": dev[1]}, device_id_type=pl.DeviceIdType.MESH)


def greet(peers):
    barrier = pltpu.get_barrier_semaphore()
    for seq, dp in peers:
        pl.semaphore_signal(barrier, inc=1, device_id={"seq": seq, "dp": dp},
                            device_id_type=pl.DeviceIdType.MESH)
    pl.semaphore_wait(barrier, len(peers))


def blk(i, w):
    return pl.ds(pl.multiple_of(i * w, w), w)


def body(q_in, g_in, k_in, v_in, n_in, start_ref, len_ref,
         dq_out, kg_out, vg_out, w_out,
         q_ref, g_ref, kv, nbuf, s_ref, d_ref, dk_ref, dv_ref, dq_ref,
         csend, crx, ysend, yrx, acc0, acc1, zsend, zrx, kga,
         w1s, w1r, w1o, nt, kt_ref, st, fac, dlt, dqa, w2s, w2r, w3s, w4r,
         s1, s3, kx_r, qx_r, kz_r, ky_r, kc_r, n_s, n_r, nf_s, nf_r, nc_s, nc_r, dq_s, dq_r,
         c_r, y_r, z_r, kc2_r, ko_r, w1_r, w2_r, w4_s, w4_r, l_sem, nl_sem, dql_sem):
    s, yl, zh, x, c, zl = coords()
    y = s * 2 + yl
    z = zh * 4 + zl
    me8 = x * 2 + c

    def dev(s_=None, yl_=None, zh_=None, x_=None, c_=None, zl_=None):
        return (seq_of(s if s_ is None else s_, yl if yl_ is None else yl_, zh if zh_ is None else zh_,
                       x if x_ is None else x_, c if c_ is None else c_), zl if zl_ is None else zl_)

    row8 = [lax.rem(me8 + d, 8) for d in range(1, 8)]
    xs = [lax.rem(x + d, 4) for d in range(1, 4)]
    ys = [lax.rem(y + d, 4) for d in range(1, 4)]
    zs = [lax.rem(z + d, 8) for d in range(1, 8)]
    ydev = [dev(s_=p // 2, yl_=lax.rem(p, 2)) for p in ys]
    zdev = [dev(zh_=p // 4, zl_=lax.rem(p, 4)) for p in zs]
    core_dev = dev(c_=1 - c)
    y_dev = dev(yl_=1 - yl)
    z_dev = dev(zh_=1 - zh)
    greet([dev(x_=p // 2, c_=lax.rem(p, 2)) for p in row8] + ydev + zdev)

    sent = {}

    def go(cp, key, kb):
        cp.start()
        sent[key] = sent.get(key, 0) + kb
        return cp

    def kib(n):
        return s_ref.at[0, pl.ds(0, n)]

    def drain(sem, n):
        rcopy(kib(n), kib(n), sem, sem, (seq_of(s, yl, zh, x, 1 - c), zl)).wait_send()

    def got(sem, n):
        rcopy(kib(n), kib(n), sem, sem, (seq_of(s, yl, zh, x, 1 - c), zl)).wait_recv()

    crow = blk(c, 128)
    last = yl * zh

    def slot(yl_, zh_, plane):
        return jnp.where(yl_ == 0, jnp.where(zh_ == plane, 0, 1), 2 + zh_)

    mine = slot(yl, zh, zh)
    for i, px in enumerate(xs):
        go(rcopy(k_in.at[0, :, blk(px, 128)], kv.at[mine, x, crow, pl.ds(0, 128)], s1, kx_r.at[i], dev(x_=px)), 1, 32)
        go(rcopy(v_in.at[0, :, blk(px, 128)], kv.at[mine, x, crow, pl.ds(128, 128)], s1, kx_r.at[i], dev(x_=px)), 1, 32)
    own_kv = [pltpu.make_async_copy(k_in.at[0, :, blk(x, 128)], kv.at[mine, x, crow, pl.ds(0, 128)], l_sem.at[0]),
              pltpu.make_async_copy(v_in.at[0, :, blk(x, 128)], kv.at[mine, x, crow, pl.ds(128, 128)], l_sem.at[1])]
    own_q = [pltpu.make_async_copy(q_in.at[0, :, blk(x, 512)], q_ref.at[x], l_sem.at[2]),
             pltpu.make_async_copy(g_in.at[0, :, blk(x, 512)], g_ref.at[x], l_sem.at[3])]
    for cp in own_kv + own_q:
        cp.start()

    def q_send(ph):
        for i, px in enumerate(xs):
            src = pl.ds(pl.multiple_of(px * 512 + ph * 256, 256), 256)
            dst = pl.ds(ph * 256, 256)
            go(rcopy(q_in.at[0, :, src], q_ref.at[x, :, dst], s1, qx_r.at[ph], dev(x_=px)), 1, 64)
            go(rcopy(g_in.at[0, :, src], g_ref.at[x, :, dst], s1, qx_r.at[ph], dev(x_=px)), 1, 64)

    q_send(0)

    def piece(sl, k):
        return kv.at[sl, lax.rem(x - k + 4, 4), crow]

    def to_core(e, k, p):
        return rcopy(p, p, s1, kc_r.at[4 * max(e - 1, 0) + k if e > 1 else e], core_dev)

    def z_copy(k):
        return rcopy(piece(mine, k), piece(slot(yl, zh, 1 - zh), k), s1, kz_r.at[k], z_dev)

    def y_copy(e, sl, k):
        return rcopy(piece(sl, k), piece(sl, k), s1, ky_r.at[4 * e + k], y_dev)

    for k in range(4):
        if k == 0:
            for cp in own_kv:
                cp.wait()
        else:
            got(kx_r.at[k - 1], 64)
        go(z_copy(k), 1, 64)
        go(y_copy(0, mine, k), 1, 64)
        go(to_core(0, k, piece(mine, k)), 1, 64)
    ev = [mine, slot(1 - yl, zh, zh), slot(yl, 1 - zh, zh), slot(1 - yl, 1 - zh, zh)]

    dk_ref[...] = jnp.zeros_like(dk_ref)
    dv_ref[...] = jnp.zeros_like(dv_ref)
    st[:, 0] = jnp.full((8, 16, 256), NEG, F32)
    st[:, 1:3] = jnp.zeros((8, 2, 16, 256), F32)
    dqa[...] = jnp.zeros_like(dqa)
    start = start_ref[s]
    end = start + len_ref[s]
    lane = lax.broadcasted_iota(jnp.int32, (1, 256), 1)

    def keys(j, n):
        if isinstance(j, int):
            return kv[j // 4, j % 4:j % 4 + n].reshape(n * 256, 256)[:, 0:128]
        return kv[j // 4, pl.ds(lax.rem(j, 4), n), :, 0:128].reshape(n * 256, 128)

    def values(j):
        return kv[j // 4, j % 4, :, 128:256]

    def rows_of(j, n=1):
        return pl.ds(j * 256 if isinstance(j, int) else pl.multiple_of(j * 256, 256), n * 256)

    def unit(u):
        h, half = u // 2, (u % 2 if isinstance(u, int) else lax.rem(u, 2))
        cols = pl.ds(h * 128 if isinstance(h, int) else pl.multiple_of(h * 128, 128), 128)
        xx = pl.ds(2 * half, 2)
        pos = yl * 2048 + zh * 1024 + (2 * half + lane // 128) * 256 + c * 128 + lax.rem(lane, 128)
        lim = jnp.maximum(start, jnp.minimum(end, pos + 1))
        return q_ref[xx, :, cols].reshape(256, 128), g_ref[xx, :, cols].reshape(256, 128), lim

    def dq_store(u, dq):
        h, half = u // 2, (u % 2 if isinstance(u, int) else lax.rem(u, 2))
        cols = pl.ds(h * 128 if isinstance(h, int) else pl.multiple_of(h * 128, 128), 128)
        dq_ref[pl.ds(2 * half, 2), :, cols] = (dq.T * SCALE).astype(BF16).reshape(2, 128, 128)

    def pass12(u, su, j, masked):
        q, g, lim = unit(u)
        rows = rows_of(j)
        sc = dot_nt(kv[j // 4, (j % 4 if isinstance(j, int) else lax.rem(j, 4)), :, 0:128], q)
        if masked:
            kpos = lax.broadcasted_iota(jnp.int32, (256, 256), 0)
            sc = jnp.where(kpos < lim - j * 256, sc, NEG)
        m = jnp.max(sc, axis=0, keepdims=True)
        e = jnp.exp2((sc - m) * EXPC)
        dp = dot_nt(kv[j // 4, (j % 4 if isinstance(j, int) else lax.rem(j, 4)), :, 128:256], g)
        st[u, 0, pl.ds(j, 1)] = m
        st[u, 1, pl.ds(j, 1)] = jnp.sum(e, axis=0, keepdims=True)
        st[u, 2, pl.ds(j, 1)] = jnp.sum(e * dp, axis=0, keepdims=True)
        s_ref[su, rows, :] = e
        d_ref[su, rows, :] = dp

    def finish(u, su):
        m = jnp.max(st[u, 0], axis=0, keepdims=True)
        f = jnp.exp2((st[u, 0] - m) * EXPC)
        f = f * (1.0 / jnp.sum(st[u, 1] * f, axis=0, keepdims=True))
        fac[su] = f
        dlt[su] = jnp.sum(st[u, 2] * f, axis=0, keepdims=True)

    def pass3(u, su, j, n, dq):
        q, g, _ = unit(u)
        dlv = dlt[su]
        ds_, p_ = [], []
        for i in range(n):
            r = rows_of(j + i)
            p = s_ref[su, r, :] * fac[su, pl.ds(j + i, 1)]
            ds_.append((p * (d_ref[su, r, :] - dlv)).astype(BF16))
            p_.append(p.astype(BF16))
        ds = ds_[0] if n == 1 else jnp.concatenate(ds_, axis=0)
        p = p_[0] if n == 1 else jnp.concatenate(p_, axis=0)
        rows = rows_of(j, n)
        dk_ref[rows, :] += dot_nn(ds, q)
        dv_ref[rows, :] += dot_nn(p, g)
        return dq + dot_nn(kt_ref[:, rows], ds)

    def arrive(e):
        sl = ev[e]

        def one(b, carry):
            j = sl * 4 + b
            kt_ref[:, rows_of(j)] = keys(j, 1).T
            for u in range(4):
                pass12(u, u, j, True)
            return carry
        lax.fori_loop(0, jnp.where(sl < 3, 4, 2 * last), one, 0)

    for k in range(4):
        y_copy(0, ev[1], k).wait_recv()
        go(to_core(1, k, piece(ev[1], k)), 1, 64)
    for cp in own_q:
        cp.wait()
    got(qx_r.at[0], 384)
    q_send(1)
    got(kc_r.at[0], 256)
    arrive(0)

    def n_copy(rr, side, cc_):
        px = lax.rem(x + (1 if side == 0 else 3), 4)
        return rcopy(n_in.at[0, :, pl.ds(pl.multiple_of(rr * 512 + cc_ * 256, 256), 256)], nbuf.at[rr, x, c],
                     n_s, n_r.at[side, rr // 4], dev(x_=px, c_=cc_))

    def n_fwd(i, side, cc_):
        rr = i + 4 * side
        src = nbuf.at[rr, lax.rem(x + (3 if side == 0 else 1), 4), cc_]
        px = lax.rem(x + (1 if side == 0 else 3), 4)
        return rcopy(src, src, nf_s, nf_r, dev(x_=px))

    def nsend(i, carry):
        for cc_ in range(2):
            n_copy(i, 0, cc_).start()
            n_copy(lax.rem(i + 4, 8), 1, cc_).start()
        mine_ = pl.ds(pl.multiple_of(i * 512 + c * 256, 256), 256)
        theirs = pl.ds(pl.multiple_of(i * 512 + (1 - c) * 256, 256), 256)
        rcopy(n_in.at[0, :, theirs], nbuf.at[i, x, c], nc_s, nc_r, core_dev).start()
        pltpu.make_async_copy(n_in.at[0, :, mine_], nbuf.at[i, x, c], nl_sem).start()
        return carry

    lax.fori_loop(0, 8, nsend, 0)
    got(kc_r.at[1], 256)
    arrive(1)

    def block(e, k):
        xb = lax.rem(x - k + 4, 4)

        @pl.when((ev[e] < 3) | ((last == 1) & (xb < 2)))
        def _():
            j = ev[e] * 4 + xb
            kt_ref[:, rows_of(j)] = keys(j, 1).T
            for u in range(4):
                pass12(u, u, j, True)

    sent[1] += 12 * 64

    def far(k, carry):
        @pl.when(k < 4)
        def _():
            z_copy(k).wait_recv()
            y_copy(1, ev[2], k).start()
            cp = to_core(2, k, piece(ev[2], k))
            cp.start()
            cp.wait_recv()
            block(2, k)

        @pl.when(k > 0)
        def _():
            y_copy(1, ev[3], k - 1).wait_recv()
            cp = to_core(3, k - 1, piece(ev[3], k - 1))
            cp.start()
            cp.wait_recv()
            block(3, k - 1)
        return carry

    lax.fori_loop(0, 5, far, 0)
    for u in range(4):
        finish(u, u)
    got(qx_r.at[1], 384)

    def mid(u, carry):
        dq = jnp.zeros((128, 256), F32)
        for j in range(12):
            dq = pass3(u, u, j, 1, dq)
            pass12(u + 4, u, j, j >= 8)
        dqa[4] = dq

        @pl.when(last == 1)
        def _():
            d2 = dqa[4]
            for j in range(12, 14):
                d2 = pass3(u, u, j, 1, d2)
                pass12(u + 4, u, j, True)
            dqa[4] = d2
        dq_store(u, dqa[4])
        finish(u + 4, u)
        return carry

    lax.fori_loop(0, 3, mid, 0)

    for side in range(2):
        got(n_r.at[side, side], 512)

    def fwd(i, carry):
        for side in range(2):
            for cc_ in range(2):
                n_fwd(i, side, cc_).start()
        return carry

    lax.fori_loop(0, 4, fwd, 0)
    lax.fori_loop(3, 4, mid, 0)

    def dq_copy(h, i):
        px = xs[i]
        return rcopy(dq_ref.at[px, :, blk(h, 128)], dq_out.at[0, :, blk(x * 4 + h, 128)],
                     dq_s, dq_r, dev(x_=px))

    def dq_local(h):
        return pltpu.make_async_copy(dq_ref.at[x, :, blk(h, 128)], dq_out.at[0, :, blk(x * 4 + h, 128)],
                                     dql_sem)

    def dq_send(h):
        for i in range(3):
            dq_copy(h, i).start()
        dq_local(h).start()

    dq_send(0)
    dq_send(1)

    def back(sl, trips):
        def two(b, carry):
            for u in range(4):
                dqa[u] = pass3(u + 4, u, sl * 4 + 2 * b, 2, dqa[u])
            return carry
        lax.fori_loop(0, trips, two, 0)

    def grads(yl_, zh_, x_, c_):
        r = pl.ds(pl.multiple_of((slot(yl_, zh_, zh) * 4 + x_) * 256 + c_ * 128, 128), 128)
        return jnp.concatenate([dk_ref[r, :] * SCALE, dv_ref[r, :]], axis=1)

    quad = [(1 - yl, 1 - zh), (yl, 1 - zh), (1 - yl, zh), (yl, zh)]
    cx = []

    def core_send(k):
        for x_ in range(4):
            csend[k, x_] = grads(quad[k][0], quad[k][1], x_, 1 - c).astype(BF16)
        cx.append(go(rcopy(csend.at[k], crx.at[k], s3, c_r.at[k], core_dev), 3, 256))

    def pair(k, x_, ch):
        r = pl.ds(pl.multiple_of((slot(quad[k][0], quad[k][1], zh) * 4 + x_) * 256 + c * 128, 128), 128)
        own = dk_ref[r, :] * SCALE if ch == 0 else dv_ref[r, :]
        return own + crx[k, x_, :, ch * 128:(ch + 1) * 128].astype(F32)

    yx = {}

    def y_stage(k, sl):
        cx[k].wait_recv()
        for ch in (1, 0):
            for x_ in range(4):
                ysend[sl, ch, x_] = pair(k, x_, ch).astype(BF16)
            yx[sl, ch] = go(rcopy(ysend.at[sl, ch], yrx.at[sl, ch], s3, y_r.at[sl, ch], y_dev), 3, 128)

    back(1, 2)
    back(2, 2 * zh)
    core_send(0)
    core_send(1)
    back(0, 2)
    y_stage(0, 0)
    cx[1].wait_recv()
    for ch in range(2):
        for x_ in range(4):
            acc1[ch, x_] = pair(1, x_, ch)
    back(2, 2 * (1 - zh))
    back(3, last)
    core_send(2)
    core_send(3)
    zx = {}
    for ch in (1, 0):
        yx[0, ch].wait_recv()
        zsend[ch] = (acc1[ch] + yrx[0, ch].astype(F32)).astype(BF16)
        zx[ch] = go(rcopy(zsend.at[ch], zrx.at[ch], s3, z_r.at[ch], z_dev), 3, 128)
    y_stage(2, 1)
    for u in range(4):
        dq_store(u + 4, dqa[u])
    dq_send(2)
    dq_send(3)
    cx[3].wait_recv()
    for ch in range(2):
        for x_ in range(4):
            acc0[ch, x_] = pair(3, x_, ch)
    for ch in (1, 0):
        yx[1, ch].wait_recv()
        acc0[ch] = acc0[ch] + yrx[1, ch].astype(F32)

    for side in range(2):
        got(n_r.at[side, 1 - side], 512)
    got(nf_r, 1024)
    got(nc_r, 512)
    pltpu.make_async_copy(kib(512), d_ref.at[0, pl.ds(0, 512)], nl_sem).wait()

    def turn(i, carry):
        nt[i] = nbuf[i].reshape(1024, 256).T
        return carry

    lax.fori_loop(0, 8, turn, 0)

    border = [1 - zh, zh]
    ko_own = []

    def final_half(ch):
        zx[ch].wait_recv()
        kga[ch, :, pl.ds(c, 1)] = (acc0[ch] + zrx[ch].astype(F32)).astype(BF16).reshape(4, 1, 128, 128)
        own = kga.at[ch, :, c]
        k2 = go(rcopy(own, own, s3, kc2_r.at[ch], core_dev), 3, 128)
        out = kg_out if ch == 0 else vg_out
        for i, px in enumerate(xs):
            go(rcopy(kga.at[ch, px, c], out.at[0, :, blk(x, 128)], s3, ko_r, dev(x_=px)), 3, 32)
        cp = pltpu.make_async_copy(kga.at[ch, x, c], out.at[0, :, blk(x, 128)], l_sem.at[4 + ch])
        cp.start()
        ko_own.append(cp)
        k2.wait_recv()
        kgall = kga[ch].reshape(1024, 128)
        for bi, b in enumerate(border):
            for d in range(3):
                py = lax.rem(y + d + 1, 4)
                w1s[ch, bi, d] = dot_nn(nt[py * 2 + b], kgall).astype(BF16)
                go(rcopy(w1s.at[ch, bi, d], w1r.at[ch, bi, d], s3, w1_r.at[ch, bi], ydev[d]), 3, 64)
        for bi, b in enumerate(border):
            w1o[ch, bi] = dot_nn(nt[y * 2 + b], kgall)

    def z_half(ch):
        for bi, b in enumerate(border):
            got(w1_r.at[ch, bi], 192)
            t = w1o[ch, bi]
            for d in range(3):
                t = t + w1r[ch, bi, d].astype(F32)
            w2s[ch, bi] = t.astype(BF16).reshape(4, 4, 16, 128)
            for i in range(bi, 4):
                pz = lax.rem(zl + i, 4)
                sl = i if bi == 0 else 3 + i
                go(rcopy(w2s.at[ch, bi, :, pz], w2r.at[ch, sl], s3, w2_r.at[ch], dev(zh_=b, zl_=pz)), 3, 16)

    final_half(1)
    final_half(0)
    z_half(1)
    z_half(0)
    for ch in (1, 0):
        got(w2_r.at[ch], 112)
        t = w2s[ch, 1, :, pl.ds(zl, 1)].reshape(4, 16, 128).astype(F32)
        for i in range(7):
            t = t + w2r[ch, i].astype(F32)
        w3s[:, :, ch * 128:(ch + 1) * 128] = t
    self_core = x // 2

    def w4_copy(xl, cc_):
        return rcopy(w3s.at[xl * 2 + cc_], w4r.at[x], w4_s.at[xl * 2 + cc_], w4_r.at[x],
                     dev(x_=2 * c + xl, c_=cc_))

    for xl in range(2):
        for cc_ in range(2):
            is_me = (2 * c + xl == x) & (c == cc_)

            @pl.when(is_me)
            def _():
                w4r[pl.ds(x, 1)] = w3s[xl * 2 + cc_].reshape(1, 16, 256)

            @pl.when(jnp.logical_not(is_me))
            def _():
                w4_copy(xl, cc_).start()
    for xx in range(4):
        @pl.when(jnp.logical_not((x == xx) & (c == self_core)))
        def _():
            rcopy(w3s.at[0], w4r.at[xx], w4_s.at[0], w4_r.at[xx], core_dev).wait_recv()
    for xx in range(4):
        w_out[:, xx * 128:(xx + 1) * 128] = w4r[xx, :, 0:128]
        w_out[:, 512 + xx * 128:512 + (xx + 1) * 128] = w4r[xx, :, 128:256]
    for xl in range(2):
        for cc_ in range(2):
            @pl.when(jnp.logical_not((2 * c + xl == x) & (c == cc_)))
            def _():
                w4_copy(xl, cc_).wait_send()
    drain(dq_s, 384)
    got(dq_r, 384)
    pltpu.make_async_copy(kib(128), d_ref.at[0, pl.ds(0, 128)], dql_sem).wait()
    got(ko_r, 192)
    for cp in ko_own:
        cp.wait()
    drain(n_s, 2048)
    drain(nf_s, 1024)
    drain(nc_s, 512)
    drain(s1, sent[1])
    drain(s3, sent[3])


def place(*refs):
    ins, outs, sem = refs[:4], refs[4:8], refs[8]
    cps = [pltpu.make_async_copy(a, b, sem.at[i]) for i, (a, b) in enumerate(zip(ins, outs))]
    for cp in cps:
        cp.start()
    for cp in cps:
        cp.wait()


def local(query, keys, values, out_grad, normed_input, q_start, q_len):
    dma = pltpu.SemaphoreType.DMA
    V = pltpu.VMEM
    hbm = pl.BlockSpec(memory_space=pl.ANY)
    smem = pl.BlockSpec(memory_space=pltpu.SMEM)
    outs = pl.pallas_call(
        body,
        name="attention_grads",
        out_shape=(jax.ShapeDtypeStruct((1, 128, 2048), BF16), jax.ShapeDtypeStruct((1, 128, 512), BF16),
                   jax.ShapeDtypeStruct((1, 128, 512), BF16), jax.ShapeDtypeStruct((16, 1024), F32)),
        in_specs=[hbm] * 5 + [smem] * 2,
        out_specs=[hbm] * 3 + [pl.BlockSpec(memory_space=pltpu.VMEM)],
        scratch_shapes=[
            V((4, 128, 512), BF16), V((4, 128, 512), BF16), V((4, 4, 256, 256), BF16),
            V((8, 4, 2, 128, 256), BF16),
            V((4, 3584, 256), F32), V((4, 3584, 256), F32), V((4096, 128), F32), V((4096, 128), F32),
            V((4, 128, 512), BF16),
            V((4, 4, 128, 256), BF16), V((4, 4, 128, 256), BF16),
            V((2, 2, 4, 128, 128), BF16), V((2, 2, 4, 128, 128), BF16),
            V((2, 4, 128, 128), F32), V((2, 4, 128, 128), F32), V((2, 4, 128, 128), BF16), V((2, 4, 128, 128), BF16),
            V((2, 4, 2, 128, 128), BF16),
            V((2, 2, 3, 256, 128), BF16), V((2, 2, 3, 256, 128), BF16), V((2, 2, 256, 128), F32), V((8, 256, 1024), BF16),
            V((128, 4096), BF16), V((8, 3, 16, 256), F32), V((4, 16, 256), F32), V((4, 1, 256), F32),
            V((5, 128, 256), F32), V((2, 2, 4, 4, 16, 128), BF16),
            V((2, 7, 4, 16, 128), BF16), V((4, 16, 256), F32), V((4, 16, 256), F32),
            dma, dma, dma((3,)), dma((2,)), dma((4,)), dma((8,)), dma((12,)), dma, dma((2, 2)), dma, dma, dma, dma,
            dma, dma, dma((4,)), dma((2, 2)), dma((2,)), dma((2,)), dma, dma((2, 2)), dma((2,)), dma((4,)), dma((4,)),
            dma((6,)), dma, dma,
        ],
        compiler_params=pltpu.CompilerParams(collective_id=0, has_side_effects=True, vmem_limit_bytes=60 << 20),
    )(query, out_grad, keys, values, normed_input, q_start, q_len)
    return pl.pallas_call(
        place,
        name="place_outputs",
        out_shape=[jax.ShapeDtypeStruct(o.shape, o.dtype) for o in outs],
        in_specs=[hbm] * 4,
        out_specs=[hbm] * 4,
        scratch_shapes=[dma((4,))],
    )(*outs)


def solution(mesh):
    tok = P("dp", "seq", None)
    return jax.shard_map(
        local, mesh=mesh,
        in_specs=(tok, tok, tok, tok, tok, P("dp"), P("dp")),
        out_specs=(tok, tok, tok, P(("seq", "dp"), None)),
        check_vma=False)
```

time: 105 us -> 124 us (1.18)
  Pallas kernels: 99.5 us -> 123 us
  local copies, waits for them, and re-layouts: 4.36 us -> 0 us
    pallas_call x0 -> x1, Pallas kernels: none -> 26.9 us  [local(): pl.pallas_call(place, name='place_outputs', out_shape=[jax.ShapeDtypeStru...]
    unnamed x10 -> x0, local copies, waits for them, and re-layouts: 4.36 us -> none
    pallas_call x1, Pallas kernels: 99.5 us -> 96.1 us  [local(): pl.pallas_call(body, name='attention_grads', out_shape=(jax.ShapeDtypeStr...]
where the time goes in v4:
time: 124 us
  Pallas kernels  123 us (99%)
    pallas_call x1, Pallas kernels, local(): pl.pallas_call(body, name='attention_grads', out_shape=(jax.ShapeDtypeStr...  96.1 us
    pallas_call x1, Pallas kernels, local(): pl.pallas_call(place, name='place_outputs', out_shape=[jax.ShapeDtypeStru...  26.9 us

profile of v4, /device:TPU:1, one launch (start us, length us, event | category | flops | bytes accessed | tf_op | source)
XLA Modules:
  0.0 123.9 jit_solution(7605092615694650790)
XLA Ops:
  0.6 96.1 %attention_grads.1 = (bf16[1,128,2048]{2,1,0:T(8,128)(2,1)}, bf16[1,128,512]{2,1,0:T(8,128)(2,1)}, bf16[1,128,512]{2,1,0:T(8,128)(2,1)}, f32[16,1024]{1,0:T(8,128)}) custom-call(bf16[1,128,2048]{2,1,0:T(8,128)(2,1)} %q_in.1, bf16[1,128,2048]{2,1,0:T(8,128)(2,1)} %g_in.1, bf16[1,128,512]{2,1,0:T(8,128)(2,1)} %k_in.1, bf16[1,128,512]{2,1,0:T(8,128)(2,1)} %v_in.1, ...), custom_call_target="tpu_custom_call" | custom-call | tf_op jit(solution)/shard_map/attention_grads/pallas_call | solution.py:536
  96.8 26.9 %place_outputs.1 = (bf16[1,128,2048]{2,1,0:T(8,128)(2,1)}, bf16[1,128,512]{2,1,0:T(8,128)(2,1)}, bf16[1,128,512]{2,1,0:T(8,128)(2,1)}, f32[16,1024]{1,0:T(8,128)}) custom-call(bf16[1,128,2048]{2,1,0:T(8,128)(2,1)} %get-tuple-element.8.refs_0_, bf16[1,128,512]{2,1,0:T(8,128)(2,1)} %get-tuple-element.9.refs_1_, ...), custom_call_target="tpu_custom_call" | custom-call | tf_op jit(solution)/shard_map/place_outputs/pallas_call | solution.py:562

commit v5 on v4

--- a/solution.py
+++ b/solution.py
@@ -63,9 +63,9 @@
          dq_out, kg_out, vg_out, w_out,
          q_ref, g_ref, kv, nbuf, s_ref, d_ref, dk_ref, dv_ref, dq_ref,
          csend, crx, ysend, yrx, acc0, acc1, zsend, zrx, kga,
-         w1s, w1r, w1o, nt, kt_ref, st, fac, dlt, dqa, w2s, w2r, w3s, w4r,
+         w1s, w1r, nt, kt_ref, st, fac, dlt, dqa, w2s, w2r, w3s, w4r,
          s1, s3, kx_r, qx_r, kz_r, ky_r, kc_r, n_s, n_r, nf_s, nf_r, nc_s, nc_r, dq_s, dq_r,
-         c_r, y_r, z_r, kc2_r, ko_r, w1_r, w2_r, w4_s, w4_r, l_sem, nl_sem, dql_sem):
+         c_r, y_r, z_s, z_r, kc2_r, ko_r, w1_r, w2_r, w4_s, w4_r, l_sem, nl_sem, dql_sem):
     s, yl, zh, x, c, zl = coords()
     y = s * 2 + yl
     z = zh * 4 + zl
@@ -132,7 +132,7 @@
         return kv.at[sl, lax.rem(x - k + 4, 4), crow]
 
     def to_core(e, k, p):
-        return rcopy(p, p, s1, kc_r.at[4 * max(e - 1, 0) + k if e > 1 else e], core_dev)
+        return rcopy(p, p, s1, kc_r.at[e], core_dev)
 
     def z_copy(k):
         return rcopy(piece(mine, k), piece(slot(yl, zh, 1 - zh), k), s1, kz_r.at[k], z_dev)
@@ -265,42 +265,25 @@
         pltpu.make_async_copy(n_in.at[0, :, mine_], nbuf.at[i, x, c], nl_sem).start()
         return carry
 
+    def far_piece(k):
+        z_copy(k).wait_recv()
+        go(y_copy(1, ev[2], k), 1, 64)
+        go(to_core(2, k, piece(ev[2], k)), 1, 64)
+
+    far_piece(0)
+    far_piece(1)
     lax.fori_loop(0, 8, nsend, 0)
     got(kc_r.at[1], 256)
     arrive(1)
-
-    def block(e, k):
-        xb = lax.rem(x - k + 4, 4)
-
-        @pl.when((ev[e] < 3) | ((last == 1) & (xb < 2)))
-        def _():
-            j = ev[e] * 4 + xb
-            kt_ref[:, rows_of(j)] = keys(j, 1).T
-            for u in range(4):
-                pass12(u, u, j, True)
-
-    sent[1] += 12 * 64
-
-    def far(k, carry):
-        @pl.when(k < 4)
-        def _():
-            z_copy(k).wait_recv()
-            y_copy(1, ev[2], k).start()
-            cp = to_core(2, k, piece(ev[2], k))
-            cp.start()
-            cp.wait_recv()
-            block(2, k)
-
-        @pl.when(k > 0)
-        def _():
-            y_copy(1, ev[3], k - 1).wait_recv()
-            cp = to_core(3, k - 1, piece(ev[3], k - 1))
-            cp.start()
-            cp.wait_recv()
-            block(3, k - 1)
-        return carry
-
-    lax.fori_loop(0, 5, far, 0)
+    far_piece(2)
+    far_piece(3)
+    for k in range(4):
+        y_copy(1, ev[3], k).wait_recv()
+        go(to_core(3, k, piece(ev[3], k)), 1, 64)
+    got(kc_r.at[2], 256)
+    arrive(2)
+    got(kc_r.at[3], 256)
+    arrive(3)
     for u in range(4):
         finish(u, u)
     got(qx_r.at[1], 384)
@@ -356,8 +339,25 @@
 
     def back(sl, trips):
         def two(b, carry):
+            j = sl * 4 + 2 * b
+            rows = rows_of(j, 2)
+            dss, ps = [], []
             for u in range(4):
-                dqa[u] = pass3(u + 4, u, sl * 4 + 2 * b, 2, dqa[u])
+                dlv = dlt[u]
+                d_, p_ = [], []
+                for i in range(2):
+                    r = rows_of(j + i)
+                    p = s_ref[u, r, :] * fac[u, pl.ds(j + i, 1)]
+                    d_.append((p * (d_ref[u, r, :] - dlv)).astype(BF16))
+                    p_.append(p.astype(BF16))
+                ds = jnp.concatenate(d_, axis=0)
+                dss.append(ds)
+                ps.append(jnp.concatenate(p_, axis=0))
+                dqa[u] += dot_nn(kt_ref[:, rows], ds)
+            q4 = jnp.concatenate([unit(u + 4)[0] for u in range(4)], axis=0)
+            g4 = jnp.concatenate([unit(u + 4)[1] for u in range(4)], axis=0)
+            dk_ref[rows, :] += dot_nn(jnp.concatenate(dss, axis=1), q4)
+            dv_ref[rows, :] += dot_nn(jnp.concatenate(ps, axis=1), g4)
             return carry
         lax.fori_loop(0, trips, two, 0)
 
@@ -402,10 +402,14 @@
     core_send(2)
     core_send(3)
     zx = {}
-    for ch in (1, 0):
+
+    def z_stage(ch):
         yx[0, ch].wait_recv()
         zsend[ch] = (acc1[ch] + yrx[0, ch].astype(F32)).astype(BF16)
-        zx[ch] = go(rcopy(zsend.at[ch], zrx.at[ch], s3, z_r.at[ch], z_dev), 3, 128)
+        zx[ch] = rcopy(zsend.at[ch], zrx.at[ch], z_s.at[ch], z_r.at[ch], z_dev)
+        zx[ch].start()
+
+    z_stage(1)
     y_stage(2, 1)
     for u in range(4):
         dq_store(u + 4, dqa[u])
@@ -419,6 +423,8 @@
         yx[1, ch].wait_recv()
         acc0[ch] = acc0[ch] + yrx[1, ch].astype(F32)
 
+    zx[1].wait_send()
+    z_stage(0)
     for side in range(2):
         got(n_r.at[side, 1 - side], 512)
     got(nf_r, 1024)
@@ -447,20 +453,17 @@
         ko_own.append(cp)
         k2.wait_recv()
         kgall = kga[ch].reshape(1024, 128)
+        w1s[ch] = dot_nn(nt[...].reshape(2048, 1024), kgall).astype(BF16).reshape(4, 2, 256, 128)
+        for d in range(3):
+            py = lax.rem(y + d + 1, 4)
+            go(rcopy(w1s.at[ch, py], w1r.at[ch, d], s3, w1_r.at[ch], ydev[d]), 3, 128)
+
+    def z_half(ch):
+        got(w1_r.at[ch], 384)
         for bi, b in enumerate(border):
+            t = w1s[ch, y, b].astype(F32)
             for d in range(3):
-                py = lax.rem(y + d + 1, 4)
-                w1s[ch, bi, d] = dot_nn(nt[py * 2 + b], kgall).astype(BF16)
-                go(rcopy(w1s.at[ch, bi, d], w1r.at[ch, bi, d], s3, w1_r.at[ch, bi], ydev[d]), 3, 64)
-        for bi, b in enumerate(border):
-            w1o[ch, bi] = dot_nn(nt[y * 2 + b], kgall)
-
-    def z_half(ch):
-        for bi, b in enumerate(border):
-            got(w1_r.at[ch, bi], 192)
-            t = w1o[ch, bi]
-            for d in range(3):
-                t = t + w1r[ch, bi, d].astype(F32)
+                t = t + w1r[ch, d, b].astype(F32)
             w2s[ch, bi] = t.astype(BF16).reshape(4, 4, 16, 128)
             for i in range(bi, 4):
                 pz = lax.rem(zl + i, 4)
@@ -512,6 +515,7 @@
     got(ko_r, 192)
     for cp in ko_own:
         cp.wait()
+    zx[0].wait_send()
     drain(n_s, 2048)
     drain(nf_s, 1024)
     drain(nc_s, 512)
@@ -549,12 +553,12 @@
             V((2, 2, 4, 128, 128), BF16), V((2, 2, 4, 128, 128), BF16),
             V((2, 4, 128, 128), F32), V((2, 4, 128, 128), F32), V((2, 4, 128, 128), BF16), V((2, 4, 128, 128), BF16),
             V((2, 4, 2, 128, 128), BF16),
-            V((2, 2, 3, 256, 128), BF16), V((2, 2, 3, 256, 128), BF16), V((2, 2, 256, 128), F32), V((8, 256, 1024), BF16),
+            V((2, 4, 2, 256, 128), BF16), V((2, 3, 2, 256, 128), BF16), V((8, 256, 1024), BF16),
             V((128, 4096), BF16), V((8, 3, 16, 256), F32), V((4, 16, 256), F32), V((4, 1, 256), F32),
             V((5, 128, 256), F32), V((2, 2, 4, 4, 16, 128), BF16),
             V((2, 7, 4, 16, 128), BF16), V((4, 16, 256), F32), V((4, 16, 256), F32),
-            dma, dma, dma((3,)), dma((2,)), dma((4,)), dma((8,)), dma((12,)), dma, dma((2, 2)), dma, dma, dma, dma,
-            dma, dma, dma((4,)), dma((2, 2)), dma((2,)), dma((2,)), dma, dma((2, 2)), dma((2,)), dma((4,)), dma((4,)),
+            dma, dma, dma((3,)), dma((2,)), dma((4,)), dma((8,)), dma((4,)), dma, dma((2, 2)), dma, dma, dma, dma,
+            dma, dma, dma((4,)), dma((2, 2)), dma((2,)), dma((2,)), dma((2,)), dma, dma((2,)), dma((2,)), dma((4,)), dma((4,)),
             dma((6,)), dma, dma,
         ],
         compiler_params=pltpu.CompilerParams(collective_id=0, has_side_effects=True, vmem_limit_bytes=60 << 20),
@@ -563,7 +567,7 @@
         place,
         name="place_outputs",
         out_shape=[jax.ShapeDtypeStruct(o.shape, o.dtype) for o in outs],
-        in_specs=[hbm] * 4,
+        in_specs=[pl.BlockSpec(memory_space=pltpu.VMEM)] * 4,
         out_specs=[hbm] * 4,
         scratch_shapes=[dma((4,))],
     )(*outs)

time: 124 us -> 99.7 us (0.80)
  Pallas kernels: 123 us -> 98.8 us
    pallas_call x1, Pallas kernels: 26.9 us -> 2.06 us  [local(): pl.pallas_call(place, name='place_outputs', out_shape=[jax.ShapeDtypeStru...]
where the time goes in v5:
time: 99.7 us; the launch traced here: 99.6 us
  Pallas kernels  98.8 us (99%)
    pallas_call x1, Pallas kernels, local(): pl.pallas_call(body, name='attention_grads', out_shape=(jax.ShapeDtypeStr...  96.8 us
    pallas_call x1, Pallas kernels, local(): pl.pallas_call(place, name='place_outputs', out_shape=[jax.ShapeDtypeStru...  2.06 us

profile of v5, /device:TPU:1, one launch (start us, length us, event | category | flops | bytes accessed | tf_op | source)
XLA Modules:
  0.0 99.6 jit_solution(12188537405953261792)
XLA Ops:
  0.6 96.8 %attention_grads.1 = (bf16[1,128,2048]{2,1,0:T(8,128)(2,1)}, bf16[1,128,512]{2,1,0:T(8,128)(2,1)}, bf16[1,128,512]{2,1,0:T(8,128)(2,1)}, f32[16,1024]{1,0:T(8,128)}) custom-call(bf16[1,128,2048]{2,1,0:T(8,128)(2,1)} %q_in.1, bf16[1,128,2048]{2,1,0:T(8,128)(2,1)} %g_in.1, bf16[1,128,512]{2,1,0:T(8,128)(2,1)} %k_in.1, bf16[1,128,512]{2,1,0:T(8,128)(2,1)} %v_in.1, ...), custom_call_target="tpu_custom_call" | custom-call | tf_op jit(solution)/shard_map/attention_grads/pallas_call | solution.py:540
  97.4 2.1 %place_outputs.1 = (bf16[1,128,2048]{2,1,0:T(8,128)(2,1)}, bf16[1,128,512]{2,1,0:T(8,128)(2,1)}, bf16[1,128,512]{2,1,0:T(8,128)(2,1)}, f32[16,1024]{1,0:T(8,128)}) custom-call(bf16[1,128,2048]{2,1,0:T(8,128)(2,1)} %get-tuple-element.8.refs_0_, bf16[1,128,512]{2,1,0:T(8,128)(2,1)} %get-tuple-element.9.refs_1_, ...), custom_call_target="tpu_custom_call" | custom-call | tf_op jit(solution)/shard_map/place_outputs/pallas_call | solution.py:566

commit v6 on v5

--- a/solution.py
+++ b/solution.py
@@ -337,12 +337,14 @@
     dq_send(0)
     dq_send(1)
 
-    def back(sl, trips):
+    def back(sl, trips, first=0):
         def two(b, carry):
             j = sl * 4 + 2 * b
             rows = rows_of(j, 2)
-            dss, ps = [], []
+            dk = dk_ref[rows, :]
+            dv = dv_ref[rows, :]
             for u in range(4):
+                q, g, _ = unit(u + 4)
                 dlv = dlt[u]
                 d_, p_ = [], []
                 for i in range(2):
@@ -351,15 +353,13 @@
                     d_.append((p * (d_ref[u, r, :] - dlv)).astype(BF16))
                     p_.append(p.astype(BF16))
                 ds = jnp.concatenate(d_, axis=0)
-                dss.append(ds)
-                ps.append(jnp.concatenate(p_, axis=0))
+                dk = dk + dot_nn(ds, q)
+                dv = dv + dot_nn(jnp.concatenate(p_, axis=0), g)
                 dqa[u] += dot_nn(kt_ref[:, rows], ds)
-            q4 = jnp.concatenate([unit(u + 4)[0] for u in range(4)], axis=0)
-            g4 = jnp.concatenate([unit(u + 4)[1] for u in range(4)], axis=0)
-            dk_ref[rows, :] += dot_nn(jnp.concatenate(dss, axis=1), q4)
-            dv_ref[rows, :] += dot_nn(jnp.concatenate(ps, axis=1), g4)
+            dk_ref[rows, :] = dk
+            dv_ref[rows, :] = dv
             return carry
-        lax.fori_loop(0, trips, two, 0)
+        lax.fori_loop(first, trips, two, 0)
 
     def grads(yl_, zh_, x_, c_):
         r = pl.ds(pl.multiple_of((slot(yl_, zh_, zh) * 4 + x_) * 256 + c_ * 128, 128), 128)
@@ -391,16 +391,14 @@
     back(2, 2 * zh)
     core_send(0)
     core_send(1)
-    back(0, 2)
+    back(0, 1)
     y_stage(0, 0)
+    back(0, 2, 1)
     cx[1].wait_recv()
     for ch in range(2):
         for x_ in range(4):
             acc1[ch, x_] = pair(1, x_, ch)
     back(2, 2 * (1 - zh))
-    back(3, last)
-    core_send(2)
-    core_send(3)
     zx = {}
 
     def z_stage(ch):
@@ -410,6 +408,9 @@
         zx[ch].start()
 
     z_stage(1)
+    back(3, last)
+    core_send(2)
+    core_send(3)
     y_stage(2, 1)
     for u in range(4):
         dq_store(u + 4, dqa[u])

time: 99.7 us -> 101 us (1.013)
  Pallas kernels: 98.8 us -> 100 us
    pallas_call x1, Pallas kernels: 96.8 us -> 98.2 us  [local(): pl.pallas_call(body, name='attention_grads', out_shape=(jax.ShapeDtypeStr...]
where the time goes in v6:
time: 101 us
  Pallas kernels  100 us (99%)
    pallas_call x1, Pallas kernels, local(): pl.pallas_call(body, name='attention_grads', out_shape=(jax.ShapeDtypeStr...  98.2 us
    pallas_call x1, Pallas kernels, local(): pl.pallas_call(place, name='place_outputs', out_shape=[jax.ShapeDtypeStru...  2.06 us

profile of v6, /device:TPU:1, one launch (start us, length us, event | category | flops | bytes accessed | tf_op | source)
XLA Modules:
  0.0 101.0 jit_solution(13196132992540046537)
XLA Ops:
  0.6 98.2 %attention_grads.1 = (bf16[1,128,2048]{2,1,0:T(8,128)(2,1)}, bf16[1,128,512]{2,1,0:T(8,128)(2,1)}, bf16[1,128,512]{2,1,0:T(8,128)(2,1)}, f32[16,1024]{1,0:T(8,128)}) custom-call(bf16[1,128,2048]{2,1,0:T(8,128)(2,1)} %q_in.1, bf16[1,128,2048]{2,1,0:T(8,128)(2,1)} %g_in.1, bf16[1,128,512]{2,1,0:T(8,128)(2,1)} %k_in.1, bf16[1,128,512]{2,1,0:T(8,128)(2,1)} %v_in.1, ...), custom_call_target="tpu_custom_call" | custom-call | tf_op jit(solution)/shard_map/attention_grads/pallas_call | solution.py:541
  98.8 2.1 %place_outputs.1 = (bf16[1,128,2048]{2,1,0:T(8,128)(2,1)}, bf16[1,128,512]{2,1,0:T(8,128)(2,1)}, bf16[1,128,512]{2,1,0:T(8,128)(2,1)}, f32[16,1024]{1,0:T(8,128)}) custom-call(bf16[1,128,2048]{2,1,0:T(8,128)(2,1)} %get-tuple-element.8.refs_0_, bf16[1,128,512]{2,1,0:T(8,128)(2,1)} %get-tuple-element.9.refs_1_, ...), custom_call_target="tpu_custom_call" | custom-call | tf_op jit(solution)/shard_map/place_outputs/pallas_call | solution.py:567

commit v7 on v6

--- a/solution.py
+++ b/solution.py
@@ -391,14 +391,16 @@
     back(2, 2 * zh)
     core_send(0)
     core_send(1)
-    back(0, 1)
+    back(0, 2)
     y_stage(0, 0)
-    back(0, 2, 1)
     cx[1].wait_recv()
     for ch in range(2):
         for x_ in range(4):
             acc1[ch, x_] = pair(1, x_, ch)
     back(2, 2 * (1 - zh))
+    back(3, last)
+    core_send(2)
+    core_send(3)
     zx = {}
 
     def z_stage(ch):
@@ -408,9 +410,6 @@
         zx[ch].start()
 
     z_stage(1)
-    back(3, last)
-    core_send(2)
-    core_send(3)
     y_stage(2, 1)
     for u in range(4):
         dq_store(u + 4, dqa[u])
@@ -455,7 +454,7 @@
         k2.wait_recv()
         kgall = kga[ch].reshape(1024, 128)
         w1s[ch] = dot_nn(nt[...].reshape(2048, 1024), kgall).astype(BF16).reshape(4, 2, 256, 128)
-        for d in range(3):
+        for d in (1, 0, 2):
             py = lax.rem(y + d + 1, 4)
             go(rcopy(w1s.at[ch, py], w1r.at[ch, d], s3, w1_r.at[ch], ydev[d]), 3, 128)
 

time: 101 us -> 97.1 us (0.961)
  Pallas kernels: 100 us -> 96.1 us
    pallas_call x1, Pallas kernels: 98.2 us -> 94.1 us  [local(): pl.pallas_call(body, name='attention_grads', out_shape=(jax.ShapeDtypeStr...]
where the time goes in v7:
time: 97.1 us; the launch traced here: 96.9 us
  Pallas kernels  96.1 us (99%)
    pallas_call x1, Pallas kernels, local(): pl.pallas_call(body, name='attention_grads', out_shape=(jax.ShapeDtypeStr...  94.1 us
    pallas_call x1, Pallas kernels, local(): pl.pallas_call(place, name='place_outputs', out_shape=[jax.ShapeDtypeStru...  2.06 us

profile of v7, /device:TPU:1, one launch (start us, length us, event | category | flops | bytes accessed | tf_op | source)
XLA Modules:
  0.0 96.9 jit_solution(2732345580639291929)
XLA Ops:
  0.6 94.1 %attention_grads.1 = (bf16[1,128,2048]{2,1,0:T(8,128)(2,1)}, bf16[1,128,512]{2,1,0:T(8,128)(2,1)}, bf16[1,128,512]{2,1,0:T(8,128)(2,1)}, f32[16,1024]{1,0:T(8,128)}) custom-call(bf16[1,128,2048]{2,1,0:T(8,128)(2,1)} %q_in.1, bf16[1,128,2048]{2,1,0:T(8,128)(2,1)} %g_in.1, bf16[1,128,512]{2,1,0:T(8,128)(2,1)} %k_in.1, bf16[1,128,512]{2,1,0:T(8,128)(2,1)} %v_in.1, ...), custom_call_target="tpu_custom_call" | custom-call | tf_op jit(solution)/shard_map/attention_grads/pallas_call | solution.py:540
  94.7 2.1 %place_outputs.1 = (bf16[1,128,2048]{2,1,0:T(8,128)(2,1)}, bf16[1,128,512]{2,1,0:T(8,128)(2,1)}, bf16[1,128,512]{2,1,0:T(8,128)(2,1)}, f32[16,1024]{1,0:T(8,128)}) custom-call(bf16[1,128,2048]{2,1,0:T(8,128)(2,1)} %get-tuple-element.8.refs_0_, bf16[1,128,512]{2,1,0:T(8,128)(2,1)} %get-tuple-element.9.refs_1_, ...), custom_call_target="tpu_custom_call" | custom-call | tf_op jit(solution)/shard_map/place_outputs/pallas_call | solution.py:566

commit v8 on v7

--- a/solution.py
+++ b/solution.py
@@ -120,7 +120,7 @@
         cp.start()
 
     def q_send(ph):
-        for i, px in enumerate(xs):
+        for px in (xs[1], xs[0], xs[2]):
             src = pl.ds(pl.multiple_of(px * 512 + ph * 256, 256), 256)
             dst = pl.ds(ph * 256, 256)
             go(rcopy(q_in.at[0, :, src], q_ref.at[x, :, dst], s1, qx_r.at[ph], dev(x_=px)), 1, 64)

time: 97.1 us -> 97.2 us (level)
  no operation moved by 1% of the time
where the time goes in v8:
time: 97.2 us; the launch traced here: 97.1 us
  Pallas kernels  96.3 us (99%)
    pallas_call x1, Pallas kernels, local(): pl.pallas_call(body, name='attention_grads', out_shape=(jax.ShapeDtypeStr...  94.2 us
    pallas_call x1, Pallas kernels, local(): pl.pallas_call(place, name='place_outputs', out_shape=[jax.ShapeDtypeStru...  2.06 us

profile of v8, /device:TPU:1, one launch (start us, length us, event | category | flops | bytes accessed | tf_op | source)
XLA Modules:
  0.0 97.1 jit_solution(8904264110119658865)
XLA Ops:
  0.6 94.2 %attention_grads.1 = (bf16[1,128,2048]{2,1,0:T(8,128)(2,1)}, bf16[1,128,512]{2,1,0:T(8,128)(2,1)}, bf16[1,128,512]{2,1,0:T(8,128)(2,1)}, f32[16,1024]{1,0:T(8,128)}) custom-call(bf16[1,128,2048]{2,1,0:T(8,128)(2,1)} %q_in.1, bf16[1,128,2048]{2,1,0:T(8,128)(2,1)} %g_in.1, bf16[1,128,512]{2,1,0:T(8,128)(2,1)} %k_in.1, bf16[1,128,512]{2,1,0:T(8,128)(2,1)} %v_in.1, ...), custom_call_target="tpu_custom_call" | custom-call | tf_op jit(solution)/shard_map/attention_grads/pallas_call | solution.py:540
  94.9 2.1 %place_outputs.1 = (bf16[1,128,2048]{2,1,0:T(8,128)(2,1)}, bf16[1,128,512]{2,1,0:T(8,128)(2,1)}, bf16[1,128,512]{2,1,0:T(8,128)(2,1)}, f32[16,1024]{1,0:T(8,128)}) custom-call(bf16[1,128,2048]{2,1,0:T(8,128)(2,1)} %get-tuple-element.8.refs_0_, bf16[1,128,512]{2,1,0:T(8,128)(2,1)} %get-tuple-element.9.refs_1_, ...), custom_call_target="tpu_custom_call" | custom-call | tf_op jit(solution)/shard_map/place_outputs/pallas_call | solution.py:566
